TPU v7x, 32 devices: a whole 2x2x4 slice. The times are simulated.
32 devices in a mesh: section: 2 (over y), rows: 4 (over z), heads: 4 (over x, core).
Axes of the slice: x: 2, y: 2, z: 4, core: 2. Of those that a mesh axis runs over, the one named last changes fastest.
Arguments:
- tokens: bfloat16 [2, 2048, 4, 1024], P('section', 'heads', 'rows'), may hold values from -6 to 6
- image_lengths: int32 [2, 4, 6], P(None, 'rows'), may hold values from 64 to 576, as said below
- tile_ranks: int32 [2, 4, 6], P(None, 'rows'), may hold values from 0 to 5, each once within a row
- w_qkv: bfloat16 [1024, 3, 1024], P(None, None, 'heads'), may hold values from -0.1875 to 0.1875
- bias_qv: bfloat16 [2, 1024], P(None, 'heads'), may hold values from -3 to 3
- w_out: bfloat16 [1024, 1024], P('heads'), may hold values from -1.5 to 1.5
- bias_out: bfloat16 [1024], replicated, may hold values from -3 to 3
- w_up: bfloat16 [1024, 4096], P(None, 'heads'), may hold values from -0.1875 to 0.1875
- bias_up: bfloat16 [4096], P('heads'), may hold values from -3 to 3
- w_down: bfloat16 [4096, 1024], P('heads'), may hold values from -0.09375 to 0.09375
- bias_down: bfloat16 [1024], replicated, may hold values from -3 to 3
- ln1_gain: bfloat16 [1024], replicated, may hold values from 0.5 to 1.5
- ln1_bias: bfloat16 [1024], replicated, may hold values from -3 to 3
- ln2_gain: bfloat16 [1024], replicated, may hold values from 0.5 to 1.5
- ln2_bias: bfloat16 [1024], replicated, may hold values from -3 to 3
- grad_out: bfloat16 [2, 2048, 4, 1024], P(None, None, 'rows', ('section', 'heads')), may hold values from -6 to 6
- grad_tap: bfloat16 [2, 2048, 4, 1024], P(None, None, 'rows', ('section', 'heads')), may hold values from -6 to 6
Outputs:
- block_output: bfloat16 [2, 2048, 4, 1024], P(None, None, 'rows', ('section', 'heads'))
- input_tap: bfloat16 [2, 2048, 4, 1024], P(None, None, 'rows', ('section', 'heads'))
- grad_tokens: float32 [2, 2048, 4, 1024], P('section', 'heads', 'rows')
- grad_w_qkv: float32 [1024, 3, 1024], P(None, None, 'heads')
- grad_bias_qv: float32 [2, 1024], P(None, 'heads')
- grad_w_out: float32 [1024, 1024], P('heads')
- grad_bias_out: float32 [1024], replicated
- grad_w_up: float32 [1024, 4096], P(None, 'heads')
- grad_bias_up: float32 [4096], P('heads')
- grad_w_down: float32 [4096, 1024], P('heads')
- grad_bias_down: float32 [1024], replicated
- grad_ln1_gain: float32 [1024], replicated
- grad_ln1_bias: float32 [1024], replicated
- grad_ln2_gain: float32 [1024], replicated
- grad_ln2_bias: float32 [1024], replicated
Inputs may be any that keep to these rules, and one draw needn't show every extreme that they name: `image_lengths`: each row holds the patch counts of the 6 images of one sequence, in packing order, summing to 1920; the remaining positions of the 2048 are padding; every row has an image of exactly 576 patches and one of exactly 64. `tile_ranks`: each row is an ordering of the images 0 to 5: their places in the decoder's order.
All inputs are finite; a program needn't handle non-finite values.
Results may differ from a plain program's by a relative error of at most 0.024.
Values may be sent and summed in bfloat16 or wider, within the bound.
A program may use at most 192 MiB of HBM per device.

v0:
```python
from functools import partial

import jax
import jax.numpy as jnp
from jax import lax
from jax.sharding import PartitionSpec as P

HD = 64


EPSILON = 1e-06
MASKED = -1e30


def layer_norm(values_in, norm_gain, norm_shift):
    average = jnp.mean(values_in, axis=-1, keepdims=True)
    centred = values_in - average
    variance = jnp.mean(centred * centred, axis=-1, keepdims=True)
    return centred * lax.rsqrt(variance + EPSILON) * norm_gain + norm_shift


def gelu_exact(values_in):
    return jax.nn.gelu(values_in, approximate=False)


def image_tables(lengths, tile_order, extent):
    image_ends = jnp.cumsum(lengths)
    image_starts = image_ends - lengths
    earlier = (tile_order[None, :] < tile_order[:, None]).astype(jnp.int32)
    new_starts = jnp.sum(earlier * lengths[None, :], axis=1)
    position = jnp.arange(extent, dtype=jnp.int32)
    segment = jnp.sum((position[:, None] >= image_ends[None, :]).astype(jnp.int32), axis=1)
    inside_new = (position[:, None] >= new_starts[None, :]) & (
        position[:, None] < (new_starts + lengths)[None, :]
    )
    source = position + jnp.sum(jnp.where(inside_new, image_starts - new_starts, 0), axis=1)
    inside_old = segment[:, None] == jnp.arange(lengths.shape[0], dtype=jnp.int32)[None, :]
    target = position + jnp.sum(jnp.where(inside_old, new_starts - image_starts, 0), axis=1)
    return (segment, source, target)


def reorder_pair(first_rows, second_rows, picks):
    extent = picks.shape[-1]
    columns = jnp.arange(extent, dtype=jnp.int32)
    selector = (picks[..., None] == columns).astype(jnp.bfloat16)
    first_out = jnp.einsum(
        "hspq,hqsc->hpsc", selector, first_rows, preferred_element_type=jnp.float32
    )
    second_out = jnp.einsum(
        "hspq,hqsc->hpsc", selector, second_rows, preferred_element_type=jnp.float32
    )
    return (first_out.astype(jnp.bfloat16), second_out.astype(jnp.bfloat16))


def masked_scores(queries, key_seq, segment_rows, segment_seq):
    scores = jnp.einsum(
        "qhd,khd->hqk", queries, key_seq, preferred_element_type=jnp.float32
    ) * HD ** (-0.5)
    allowed = segment_rows[:, None] == segment_seq[None, :]
    return jnp.where(allowed[None], scores, MASKED)


def attend_forward(query_seq, key_seq, value_seq, segment_seq, block_rows):
    extent = query_seq.shape[0]
    block_count = extent // block_rows
    query_blocks = query_seq.reshape((block_count, block_rows) + query_seq.shape[1:])
    segment_blocks = segment_seq.reshape(block_count, block_rows)

    def one_block(block_item):
        queries, segment_rows = block_item
        scores = masked_scores(queries, key_seq, segment_rows, segment_seq)
        row_max = jnp.max(scores, axis=-1, keepdims=True)
        exponent = jnp.exp(scores - row_max)
        row_total = jnp.sum(exponent, axis=-1, keepdims=True)
        attend_prob = (exponent / row_total).astype(jnp.bfloat16)
        mixture = jnp.einsum(
            "hqk,khd->qhd", attend_prob, value_seq, preferred_element_type=jnp.float32
        )
        return (mixture, (row_max + jnp.log(row_total))[..., 0])

    mixture, log_sum = lax.map(one_block, (query_blocks, segment_blocks))
    return (mixture.reshape(query_seq.shape), log_sum)


def attend_backward(query_seq, key_seq, value_seq, segment_seq, log_sum, grad_seq, block_rows):
    extent = query_seq.shape[0]
    block_count = extent // block_rows
    query_blocks = query_seq.reshape((block_count, block_rows) + query_seq.shape[1:])
    grad_blocks = grad_seq.reshape((block_count, block_rows) + grad_seq.shape[1:])
    segment_blocks = segment_seq.reshape(block_count, block_rows)

    def one_block(running, block_item):
        key_acc, value_acc = running
        queries, segment_rows, log_rows, grad_rows = block_item
        scores = masked_scores(queries, key_seq, segment_rows, segment_seq)
        attend_prob = jnp.exp(scores - log_rows[..., None])
        prob_low = attend_prob.astype(jnp.bfloat16)
        grad_prob = jnp.einsum(
            "qhd,khd->hqk", grad_rows, value_seq, preferred_element_type=jnp.float32
        )
        inner = jnp.sum(attend_prob * grad_prob, axis=-1, keepdims=True)
        grad_score = (attend_prob * (grad_prob - inner) * HD ** (-0.5)).astype(jnp.bfloat16)
        grad_query = jnp.einsum(
            "hqk,khd->qhd", grad_score, key_seq, preferred_element_type=jnp.float32
        )
        key_acc = key_acc + jnp.einsum(
            "hqk,qhd->khd", grad_score, queries, preferred_element_type=jnp.float32
        )
        value_acc = value_acc + jnp.einsum(
            "hqk,qhd->khd", prob_low, grad_rows, preferred_element_type=jnp.float32
        )
        return ((key_acc, value_acc), grad_query)

    zero_rows = jnp.zeros(key_seq.shape, jnp.float32)
    (grad_key, grad_value), grad_query = lax.scan(
        one_block, (zero_rows, zero_rows), (query_blocks, segment_blocks, log_sum, grad_blocks)
    )
    return (grad_query.reshape(query_seq.shape), grad_key, grad_value)


def per_device(
    tokens,
    image_lengths,
    tile_ranks,
    w_qkv,
    bias_qv,
    w_out,
    bias_out,
    w_up,
    bias_up,
    w_down,
    bias_down,
    ln1_gain,
    ln1_bias,
    ln2_gain,
    ln2_bias,
    grad_out,
    grad_tap,
):
    own_tokens = tokens[0]
    part_rows = own_tokens.shape[0]
    seq_count = own_tokens.shape[1]
    full_len = part_rows * lax.axis_size("heads")
    block_rows = min(512, full_len)
    section_at = lax.axis_index("section")
    head_at = lax.axis_index("heads")
    halves = image_lengths.shape[0]
    image_count = image_lengths.shape[2]
    flat_lengths = image_lengths.reshape(halves * seq_count, image_count)
    flat_orders = tile_ranks.reshape(halves * seq_count, image_count)
    segments, sources, targets = jax.vmap(partial(image_tables, extent=full_len))(
        flat_lengths, flat_orders
    )
    segments = segments.reshape(halves, seq_count, full_len)
    sources = sources.reshape(halves, seq_count, full_len)
    targets = targets.reshape(halves, seq_count, full_len)
    own_segments = lax.dynamic_index_in_dim(segments, section_at, 0, keepdims=False)
    row_places = head_at * part_rows + jnp.arange(part_rows, dtype=jnp.int32)
    valid_rows = (
        (jnp.take(own_segments, row_places, axis=1) < image_count).astype(jnp.float32).T[:, :, None]
    )
    token_values = own_tokens.astype(jnp.float32)
    normed_one = layer_norm(token_values, ln1_gain, ln1_bias).astype(jnp.bfloat16)
    gathered_one = lax.all_gather(normed_one, "heads", axis=0, tiled=True)
    projected = jnp.einsum("rsd,dck->rsck", gathered_one, w_qkv, preferred_element_type=jnp.float32)
    query_all = (projected[:, :, 0] + bias_qv[0]).astype(jnp.bfloat16)
    key_all = projected[:, :, 1].astype(jnp.bfloat16)
    value_all = (projected[:, :, 2] + bias_qv[1]).astype(jnp.bfloat16)
    head_groups = query_all.shape[2] // HD
    split_shape = (full_len, seq_count, head_groups, HD)
    query_heads = query_all.reshape(split_shape)
    key_heads = key_all.reshape(split_shape)
    value_heads = value_all.reshape(split_shape)
    which = 0
    mixture, log_sum = attend_forward(
        query_heads[:, which],
        key_heads[:, which],
        value_heads[:, which],
        own_segments[which],
        block_rows,
    )
    mixtures = [mixture]
    log_sums = [log_sum]
    attended = (
        jnp.stack(mixtures, axis=1)
        .reshape(full_len, seq_count, head_groups * HD)
        .astype(jnp.bfloat16)
    )
    picked = attended
    attn_sum = (
        lax.psum_scatter(
            jnp.einsum("rsk,kd->rsd", picked, w_out, preferred_element_type=jnp.float32).astype(
                jnp.bfloat16
            ),
            "heads",
            scatter_dimension=0,
            tiled=True,
        ).astype(jnp.float32)
        + bias_out
    )
    after_attn = token_values + attn_sum
    normed_two = layer_norm(after_attn, ln2_gain, ln2_bias).astype(jnp.bfloat16)
    gathered_two = lax.all_gather(normed_two, "heads", axis=0, tiled=True)
    pre_act = (
        jnp.einsum("rsd,df->rsf", gathered_two, w_up, preferred_element_type=jnp.float32) + bias_up
    )
    activated = gelu_exact(pre_act).astype(jnp.bfloat16)
    picked = activated
    mlp_sum = (
        lax.psum_scatter(
            jnp.einsum("rsf,fd->rsd", picked, w_down, preferred_element_type=jnp.float32).astype(
                jnp.bfloat16
            ),
            "heads",
            scatter_dimension=0,
            tiled=True,
        ).astype(jnp.float32)
        + bias_down
    )
    block_out = ((after_attn + mlp_sum) * valid_rows).astype(jnp.bfloat16)
    sent_out, sent_tap = (
        lax.all_to_all(block_out, ("section", "heads"), split_axis=2, concat_axis=0, tiled=True),
        lax.all_to_all(own_tokens, ("section", "heads"), split_axis=2, concat_axis=0, tiled=True),
    )
    decoder_shape = (halves, full_len, seq_count, sent_out.shape[2])
    output_dec, tap_dec = reorder_pair(
        sent_out.reshape(decoder_shape), sent_tap.reshape(decoder_shape), sources
    )
    encoder_shape = (halves * full_len, seq_count, grad_out.shape[3])
    back_out, back_tap = reorder_pair(grad_out, grad_tap, targets)
    grad_block, grad_direct = (
        lax.all_to_all(
            back_out.reshape(encoder_shape),
            ("section", "heads"),
            split_axis=0,
            concat_axis=2,
            tiled=True,
        ),
        lax.all_to_all(
            back_tap.reshape(encoder_shape),
            ("section", "heads"),
            split_axis=0,
            concat_axis=2,
            tiled=True,
        ),
    )
    grad_mlp_full = grad_block.astype(jnp.float32) * valid_rows
    grad_mlp = grad_mlp_full.astype(jnp.bfloat16)
    grad_b_down = jnp.sum(grad_mlp, axis=(0, 1), dtype=jnp.float32)
    grad_mlp_all = lax.all_gather(grad_mlp, "heads", axis=0, tiled=True)
    grad_w_down_part = jnp.einsum(
        "rsf,rsd->fd", activated, grad_mlp_all, preferred_element_type=jnp.float32
    )
    grad_act = jnp.einsum("rsd,fd->rsf", grad_mlp_all, w_down, preferred_element_type=jnp.float32)
    gelu_back = jax.vjp(gelu_exact, pre_act)[1]
    grad_pre = gelu_back(grad_act)[0].astype(jnp.bfloat16)
    grad_w_up_part = jnp.einsum(
        "rsd,rsf->df", gathered_two, grad_pre, preferred_element_type=jnp.float32
    )
    grad_b_up = jnp.sum(grad_pre, axis=(0, 1), dtype=jnp.float32)
    picked = grad_pre
    grad_normed_two = lax.psum_scatter(
        jnp.einsum("rsf,df->rsd", picked, w_up, preferred_element_type=jnp.float32).astype(
            jnp.bfloat16
        ),
        "heads",
        scatter_dimension=0,
        tiled=True,
    ).astype(jnp.float32)
    norm_two_back = jax.vjp(layer_norm, after_attn, ln2_gain, ln2_bias)[1]
    grad_after, grad_gain_two, grad_shift_two = norm_two_back(grad_normed_two)
    grad_after = grad_after + grad_mlp_full
    grad_attn = grad_after.astype(jnp.bfloat16)
    grad_b_out = jnp.sum(grad_attn, axis=(0, 1), dtype=jnp.float32)
    grad_attn_all = lax.all_gather(grad_attn, "heads", axis=0, tiled=True)
    grad_w_out_part = jnp.einsum(
        "rsk,rsd->kd", attended, grad_attn_all, preferred_element_type=jnp.float32
    )
    grad_attended = (
        jnp.einsum("rsd,kd->rsk", grad_attn_all, w_out, preferred_element_type=jnp.float32)
        .astype(jnp.bfloat16)
        .reshape(split_shape)
    )
    which = 0
    grad_query, grad_key, grad_value = attend_backward(
        query_heads[:, which],
        key_heads[:, which],
        value_heads[:, which],
        own_segments[which],
        log_sums[which],
        grad_attended[:, which],
        block_rows,
    )
    query_grads = [grad_query]
    key_grads = [grad_key]
    value_grads = [grad_value]
    flat_shape = (full_len, seq_count, head_groups * HD)
    grad_query_all = jnp.stack(query_grads, axis=1).reshape(flat_shape).astype(jnp.bfloat16)
    grad_key_all = jnp.stack(key_grads, axis=1).reshape(flat_shape).astype(jnp.bfloat16)
    grad_value_all = jnp.stack(value_grads, axis=1).reshape(flat_shape).astype(jnp.bfloat16)
    grad_projected = jnp.stack([grad_query_all, grad_key_all, grad_value_all], axis=2)
    grad_w_qkv_part = jnp.einsum(
        "rsd,rsck->dck", gathered_one, grad_projected, preferred_element_type=jnp.float32
    )
    grad_b_qv = jnp.stack(
        [
            jnp.sum(grad_query_all, axis=(0, 1), dtype=jnp.float32),
            jnp.sum(grad_value_all, axis=(0, 1), dtype=jnp.float32),
        ]
    )
    picked = grad_projected
    grad_normed_one = lax.psum_scatter(
        jnp.einsum("rsck,dck->rsd", picked, w_qkv, preferred_element_type=jnp.float32).astype(
            jnp.bfloat16
        ),
        "heads",
        scatter_dimension=0,
        tiled=True,
    ).astype(jnp.float32)
    norm_one_back = jax.vjp(layer_norm, token_values, ln1_gain, ln1_bias)[1]
    grad_input, grad_gain_one, grad_shift_one = norm_one_back(grad_normed_one)
    grad_tokens = grad_input + grad_after + grad_direct.astype(jnp.float32)
    (
        grad_w_qkv_part,
        grad_b_qv,
        grad_w_out_part,
        grad_b_out,
        grad_gain_one,
        grad_shift_one,
        grad_w_up_part,
        grad_b_up,
        grad_w_down_part,
        grad_b_down,
        grad_gain_two,
        grad_shift_two,
    ) = (
        lax.psum(grad_w_qkv_part.astype(jnp.bfloat16), ("section", "rows")).astype(jnp.float32),
        lax.psum(grad_b_qv.astype(jnp.bfloat16), ("section", "rows")).astype(jnp.float32),
        lax.psum(grad_w_out_part.astype(jnp.bfloat16), ("section", "rows")).astype(jnp.float32),
        lax.psum(grad_b_out.astype(jnp.bfloat16), ("section", "rows")).astype(jnp.float32),
        lax.psum(grad_gain_one, ("section", "rows")).astype(jnp.float32),
        lax.psum(grad_shift_one, ("section", "rows")).astype(jnp.float32),
        lax.psum(grad_w_up_part.astype(jnp.bfloat16), ("section", "rows")).astype(jnp.float32),
        lax.psum(grad_b_up.astype(jnp.bfloat16), ("section", "rows")).astype(jnp.float32),
        lax.psum(grad_w_down_part.astype(jnp.bfloat16), ("section", "rows")).astype(jnp.float32),
        lax.psum(grad_b_down.astype(jnp.bfloat16), ("section", "rows")).astype(jnp.float32),
        lax.psum(grad_gain_two, ("section", "rows")).astype(jnp.float32),
        lax.psum(grad_shift_two, ("section", "rows")).astype(jnp.float32),
    )
    grad_b_out, grad_b_down, grad_gain_one, grad_shift_one, grad_gain_two, grad_shift_two = (
        lax.psum(
            (grad_b_out, grad_b_down, grad_gain_one, grad_shift_one, grad_gain_two, grad_shift_two),
            "heads",
        )
    )
    return (
        output_dec,
        tap_dec,
        grad_tokens[None],
        grad_w_qkv_part,
        grad_b_qv,
        grad_w_out_part,
        grad_b_out,
        grad_w_up_part,
        grad_b_up,
        grad_w_down_part,
        grad_b_down,
        grad_gain_one,
        grad_shift_one,
        grad_gain_two,
        grad_shift_two,
    )


def solution(mesh):
    placed = (
        P("section", "heads", "rows", None),
        P(None, "rows", None),
        P(None, "rows", None),
        P(None, None, "heads"),
        P(None, "heads"),
        P("heads", None),
        P(),
        P(None, "heads"),
        P("heads"),
        P("heads", None),
        P(),
        P(),
        P(),
        P(),
        P(),
        P(None, None, "rows", ("section", "heads")),
        P(None, None, "rows", ("section", "heads")),
    )
    return jax.shard_map(
        per_device,
        mesh=mesh,
        in_specs=placed,
        out_specs=(
            P(None, None, "rows", ("section", "heads")),
            P(None, None, "rows", ("section", "heads")),
            P("section", "heads", "rows", None),
            P(None, None, "heads"),
            P(None, "heads"),
            P("heads", None),
            P(),
            P(None, "heads"),
            P("heads"),
            P("heads", None),
            P(),
            P(),
            P(),
            P(),
            P(),
        ),
        check_vma=False,
    )
```

profile of v0, /device:TPU:0, one launch (start us, length us, event | category | flops | bytes accessed | tf_op | source)
XLA Modules:
  0.0 1077.3 jit_solution(13621030071722300098)
XLA Ops:
  17.5 35.0 %all-gather.5.cloned.1.call-done = bf16[2048,1,1024]{2,0,1:T(8,128)(2,1)} async-done(((bf16[512,1,1024]{2,0,1:T(8,128)(2,1)}), bf16[2048,1,1024]{2,0,1:T(8,128)(2,1)}) %all-gather.5.cloned.1.call-update) | async-done | bytes 4194320 | tf_op jit(solution)/shard_map/all_gather | solution.py:164
  52.5 5.8 fusion.115
  69.9 62.9 %while.27 = (s32[]{:T(128)}, bf16[4,512,4,64]{1,3,2,0:T(8,128)(2,1)}, f32[4,4,512]{2,1,0:T(4,128)}, s32[4,512]{1,0:T(4,128)S(1)}, s32[1,2048]{1,0:T(1,128)S(1)},...) while((s32[]{:T(128)}, ...), condition=%wide.region_7.8_spmd, body=%wide.region_4.7_spmd.sunk | while | flops 1125120000 | bytes 70072528 | solution.py:81
  70.6 4.5 fusion.230
  75.1 4.4 fusion.231
  79.6 5.1 fusion.232
  86.3 4.5 fusion.230
  90.8 4.4 fusion.231
  95.3 5.1 fusion.232
  102.0 4.5 fusion.230
  106.5 4.4 fusion.231
  111.0 5.1 fusion.232
  117.7 4.5 fusion.230
  122.2 4.4 fusion.231
  126.6 5.1 fusion.232
  139.8 44.5 %reduce-scatter.5.cloned.1.call-done = bf16[512,1,1024]{2,0,1:T(8,128)(2,1)} async-done(((bf16[2048,1,1024]{2,0,1:T(8,128)(2,1)}), bf16[512,1,1024]{2,0,1:T(8,128)(2,1)}) %reduce-scatter.5.cloned.1.call-update) | async-done | bytes 1048592 | tf_op jit(solution)/shard_map/reduce_scatter | solution.py:191
  191.5 7.9 fusion.130
  212.9 22.5 %all-to-all-done.2 = bf16[8,2,32768]{2,1,0:T(2,128)(2,1)} async-done(((bf16[8,2,32768]{2,1,0:T(2,128)(2,1)}), bf16[8,2,32768]{2,1,0:T(2,128)(2,1)}, u32[]{:S(2)}, u32[]{:S(2)}) %all-to-all-start.2) | async-done | bytes 1048608 | tf_op jit(solution)/shard_map/all_to_all | solution.py:232
  235.4 5.8 reshape.983
  245.8 26.1 %multiply_convert_fusion.1 = (bf16[2048,1024]{1,0:T(8,128)(2,1)}, f32[2048,1024]{1,0:T(8,128)}, f32[2048,1024]{1,0:T(8,128)}) fusion(f32[1024]{0:T(1024)S(1)} %convert_element_type.441, bf16[1024,1024]{1,0:T(8,128)(2,1)S(1)} %copy-done, bf16[2048,1,1024]{2,0,1:T(8,128)(2,1)} %all-gather.7.cloned.1.call-done), kind=kOutput, calls=%fused_computation.81 | convolution fusion | flops 4433379328 | bytes 27267072 | tf_op jit(solution)/shard_map/rsd,df->rsf/dot_general | solution.py:205
  271.9 7.6 all-gather.9.cloned.1.call-done
  279.4 13.9 %fusion.186 = (bf16[1024]{0:T(1024)(128)(2,1)}, bf16[2048,1024]{1,0:T(8,128)(2,1)S(1)}) fusion(f32[2048,1024]{1,0:T(8,128)} %get-tuple-element.358, bf16[1024,1024]{1,0:T(8,128)(2,1)} %param.30, bf16[2048,1,1024]{2,0,1:T(8,128)(2,1)} %all-gather.9.cloned.1.call-done, f32[2048,1024]{1,0:T(8,128)} %get-tuple-element.369, f32[1024]{0:T(1024)S(1)} %convert_element_type.441), kind=kOutput, calls=%fused_computation.215 | convolution fusion | flops 4328520704 | bytes 27269120 | tf_op jit(solution)/shard_map/rsd,fd->rsf/dot_general | solution.py:254
  295.3 6.1 convert_bitcast_fusion
  303.0 8.5 convert_bitcast_fusion.1
  312.2 33.9 %reduce-scatter.9.cloned.1.call-done = bf16[512,1,1024]{2,0,1:T(8,128)(2,1)} async-done(((bf16[2048,1,1024]{2,0,1:T(8,128)(2,1)}), bf16[512,1,1024]{2,0,1:T(8,128)(2,1)}) %reduce-scatter.9.cloned.1.call-update) | async-done | bytes 1048592 | tf_op jit(solution)/shard_map/reduce_scatter | solution.py:262
  348.1 44.9 %reduce-scatter.7.cloned.1.call-done = bf16[512,1,1024]{2,0,1:T(8,128)(2,1)} async-done(((bf16[2048,1,1024]{2,0,1:T(8,128)(2,1)}), bf16[512,1,1024]{2,0,1:T(8,128)(2,1)}) %reduce-scatter.7.cloned.1.call-update) | async-done | bytes 1048592 | tf_op jit(solution)/shard_map/reduce_scatter | solution.py:210
  393.0 4.6 fusion.141
  401.0 9.5 fusion.150
  410.4 5.8 fusion.147
  416.2 19.3 %all-gather.11.cloned.1.call-done = bf16[2048,1,1024]{2,0,1:T(8,128)(2,1)} async-done(((bf16[512,1,1024]{2,0,1:T(8,128)(2,1)}), bf16[2048,1,1024]{2,0,1:T(8,128)(2,1)}) %all-gather.11.cloned.1.call-update) | async-done | bytes 4194320 | tf_op jit(solution)/shard_map/all_gather | solution.py:275
  445.9 282.8 %while.28 = (s32[]{:T(128)}, f32[2048,4,64]{0,2,1:T(8,128)}, f32[2048,4,64]{0,2,1:T(8,128)}, bf16[4,512,4,64]{1,3,2,0:T(8,128)(2,1)}, bf16[4,512,4,64]{1,3,2,0:T...) while((s32[]{:T(128)}, f32[2048,4,64]{0,2,1:T(8,128)}, ...), condition=%wide.region_20.21_spmd.clone, body=%wide.region_18.20_spmd.clone.sunk | while | flops 2796560384 | bytes 275323104 | solution.py:115
  451.2 6.8 fusion.246
  458.0 8.1 fusion.243
  466.1 24.0 %fusion.247 = bf16[4,512,4,64]{1,3,2,0:T(8,128)(2,1)} fusion(bf16[4,512,4,64]{1,3,2,0:T(8,128)(2,1)} %get-tuple-element.537, s32[]{:T(128)S(6)} %copy.184, bf16[2048,4,64]{0,2,1:T(8,128)(2,1)S(1)} %get-tuple-element.554, f32[4,512,2048]{2,1,0:T(8,128)} %fusion.243, f32[4,512,2048]{2,1,0:T(8,128)} %copy-done.2, ...), kind=kOutput, calls=%fused_computation.42.clone.1 | convolution fusion | flops 583012352 | bytes 70795264 | tf_op jit(solution)/shard_map/while/body/eval_jaxpr/hqk,khd->qhd/dot_general | solution.py:103
  490.0 25.5 %fusion.245 = f32[2048,4,64]{0,2,1:T(8,128)} fusion(f32[4,512,2048]{2,1,0:T(8,128)} %fusion.243, f32[4,512,2048]{2,1,0:T(8,128)} %copy-done.2, f32[4,512]{1,0:T(4,128)S(1)} %dynamic-slice_bitcast_fusion.2, pred[512,2048]{1,0:T(8,128)(4,1)S(1)} %broadcast_compare_fusion.5, f32[2048,4,64]{0,2,1:T(8,128)} %get-tuple-element.535, pred[]{:T(512)S(6)} %compare.3, ...), kind=kOutput, calls=%fused_computation.39.clone.1 | convolution fusion | flops 584060928 | bytes 73678856 | tf_op jit(solution)/shard_map/while/body/eval_jaxpr/hqk,qhd->khd/dot_general | solution.py:106
  520.3 8.0 fusion.246
  528.4 8.1 fusion.243
  536.5 24.0 %fusion.247 = bf16[4,512,4,64]{1,3,2,0:T(8,128)(2,1)} fusion(bf16[4,512,4,64]{1,3,2,0:T(8,128)(2,1)} %get-tuple-element.537, s32[]{:T(128)S(6)} %copy.184, bf16[2048,4,64]{0,2,1:T(8,128)(2,1)S(1)} %get-tuple-element.554, f32[4,512,2048]{2,1,0:T(8,128)} %fusion.243, f32[4,512,2048]{2,1,0:T(8,128)} %copy-done.2, ...), kind=kOutput, calls=%fused_computation.42.clone.1 | convolution fusion | flops 583012352 | bytes 70795264 | tf_op jit(solution)/shard_map/while/body/eval_jaxpr/hqk,khd->qhd/dot_general | solution.py:103
  560.5 26.1 %fusion.245 = f32[2048,4,64]{0,2,1:T(8,128)} fusion(f32[4,512,2048]{2,1,0:T(8,128)} %fusion.243, f32[4,512,2048]{2,1,0:T(8,128)} %copy-done.2, f32[4,512]{1,0:T(4,128)S(1)} %dynamic-slice_bitcast_fusion.2, pred[512,2048]{1,0:T(8,128)(4,1)S(1)} %broadcast_compare_fusion.5, f32[2048,4,64]{0,2,1:T(8,128)} %get-tuple-element.535, pred[]{:T(512)S(6)} %compare.3, ...), kind=kOutput, calls=%fused_computation.39.clone.1 | convolution fusion | flops 584060928 | bytes 73678856 | tf_op jit(solution)/shard_map/while/body/eval_jaxpr/hqk,qhd->khd/dot_general | solution.py:106
  591.3 8.0 fusion.246
  599.4 8.1 fusion.243
  607.5 24.0 %fusion.247 = bf16[4,512,4,64]{1,3,2,0:T(8,128)(2,1)} fusion(bf16[4,512,4,64]{1,3,2,0:T(8,128)(2,1)} %get-tuple-element.537, s32[]{:T(128)S(6)} %copy.184, bf16[2048,4,64]{0,2,1:T(8,128)(2,1)S(1)} %get-tuple-element.554, f32[4,512,2048]{2,1,0:T(8,128)} %fusion.243, f32[4,512,2048]{2,1,0:T(8,128)} %copy-done.2, ...), kind=kOutput, calls=%fused_computation.42.clone.1 | convolution fusion | flops 583012352 | bytes 70795264 | tf_op jit(solution)/shard_map/while/body/eval_jaxpr/hqk,khd->qhd/dot_general | solution.py:103
  631.5 26.1 %fusion.245 = f32[2048,4,64]{0,2,1:T(8,128)} fusion(f32[4,512,2048]{2,1,0:T(8,128)} %fusion.243, f32[4,512,2048]{2,1,0:T(8,128)} %copy-done.2, f32[4,512]{1,0:T(4,128)S(1)} %dynamic-slice_bitcast_fusion.2, pred[512,2048]{1,0:T(8,128)(4,1)S(1)} %broadcast_compare_fusion.5, f32[2048,4,64]{0,2,1:T(8,128)} %get-tuple-element.535, pred[]{:T(512)S(6)} %compare.3, ...), kind=kOutput, calls=%fused_computation.39.clone.1 | convolution fusion | flops 584060928 | bytes 73678856 | tf_op jit(solution)/shard_map/while/body/eval_jaxpr/hqk,qhd->khd/dot_general | solution.py:106
  662.4 8.0 fusion.246
  670.4 8.1 fusion.243
  678.5 24.0 %fusion.247 = bf16[4,512,4,64]{1,3,2,0:T(8,128)(2,1)} fusion(bf16[4,512,4,64]{1,3,2,0:T(8,128)(2,1)} %get-tuple-element.537, s32[]{:T(128)S(6)} %copy.184, bf16[2048,4,64]{0,2,1:T(8,128)(2,1)S(1)} %get-tuple-element.554, f32[4,512,2048]{2,1,0:T(8,128)} %fusion.243, f32[4,512,2048]{2,1,0:T(8,128)} %copy-done.2, ...), kind=kOutput, calls=%fused_computation.42.clone.1 | convolution fusion | flops 583012352 | bytes 70795264 | tf_op jit(solution)/shard_map/while/body/eval_jaxpr/hqk,khd->qhd/dot_general | solution.py:103
  702.5 26.1 %fusion.245 = f32[2048,4,64]{0,2,1:T(8,128)} fusion(f32[4,512,2048]{2,1,0:T(8,128)} %fusion.243, f32[4,512,2048]{2,1,0:T(8,128)} %copy-done.2, f32[4,512]{1,0:T(4,128)S(1)} %dynamic-slice_bitcast_fusion.2, pred[512,2048]{1,0:T(8,128)(4,1)S(1)} %broadcast_compare_fusion.5, f32[2048,4,64]{0,2,1:T(8,128)} %get-tuple-element.535, pred[]{:T(512)S(6)} %compare.3, ...), kind=kOutput, calls=%fused_computation.39.clone.1 | convolution fusion | flops 584060928 | bytes 73678856 | tf_op jit(solution)/shard_map/while/body/eval_jaxpr/hqk,qhd->khd/dot_general | solution.py:106
  738.6 4.4 fusion.160
  743.1 4.7 fusion.154
  749.0 7.1 fusion.118
  757.4 6.8 fusion.131
  768.0 4.7 all-to-all-start.3
  776.5 9.1 reduce.38
  788.3 4.2 all-to-all-start.1
  796.5 8.1 reduce.37
  806.1 4.5 all-to-all-done.1
  814.4 5.8 reshape.989
  822.9 5.8 reshape.987
  833.8 7.9 fusion.135
  848.4 8.6 fusion.136
  858.7 103.9 %all-reduce.5.cloned.1.call-done = (bf16[1024,3,256]{2,0,1:T(8,128)(2,1)}, bf16[256,1024]{1,0:T(8,128)(2,1)}, bf16[1024,1024]{1,0:T(8,128)(2,1)}, bf16[1024,1024]{1,0:T(8,128)(2,1)}) async-done(((bf16[1024,3,256]{2,0,1:T(8,128)(2,1)}, bf16[256,1024]{1,0:T(8,128)(2,1)}, bf16[1024,1024]{1,0:T(8,128)(2,1)}, bf16[1024,1024]{1,0:T(8,128)(2,1)}), (bf16[1024,3,256]{2,0,1:T(8,128)(2,1)}, ...) | async-done | bytes 6291472 | tf_op jit(solution)/shard_map/psum | solution.py:337
  973.6 35.0 %reduce-scatter.11.cloned.1.call-done = bf16[512,1,1024]{2,0,1:T(8,128)(2,1)} async-done(((bf16[2048,1,1024]{2,0,1:T(8,128)(2,1)}), bf16[512,1,1024]{2,0,1:T(8,128)(2,1)}) %reduce-scatter.11.cloned.1.call-update) | async-done | bytes 1048592 | tf_op jit(solution)/shard_map/reduce_scatter | solution.py:312
  1014.3 37.5 %all-reduce.1 = (bf16[1024]{0:T(1024)(128)(2,1)S(1)}, bf16[1024]{0:T(1024)(128)(2,1)S(1)}, bf16[1024]{0:T(1024)(128)(2,1)S(1)}, bf16[1024]{0:T(1024)(128)(2,1)S(...) all-reduce(bf16[1024]{0:T(1024)(128)(2,1)S(1)} %copy-done.48, ...), channel_id=1, replica_groups=mesh['section'=2,'rows'=4,'heads'=4] {'section','rows'}, use_global_device_ids=true, to_apply=%region_30.31 | all-reduce | flops 7680 | bytes 30720 | tf_op jit(solution)/shard_map/psum | solution.py:340
  1059.6 10.9 %all-reduce = (f32[1024]{0:T(1024)}, f32[1024]{0:T(1024)}, f32[1024]{0:T(1024)}, f32[1024]{0:T(1024)}, f32[1024]{0:T(1024)}, /*index=5*/f32[1024]{0:T(1024)}) all-reduce(bf16[1024]{0:T(1024)(128)(2,1)S(1)} %get-tuple-element.338, ...), channel_id=1, replica_groups=mesh['section'=2,'rows'=4,'heads'=4] {'heads'}, use_global_device_ids=true, to_apply=%region_31.32 | all-reduce | flops 6144 | bytes 36864 | tf_op jit(solution)/shard_map/psum | solution.py:351
  (313 shorter events, 172.1 us)
Async XLA Ops:
  7.2 238.6 %copy-start = (bf16[1024,1024]{1,0:T(8,128)(2,1)S(1)}, bf16[1024,1024]{1,0:T(8,128)(2,1)}, u32[]{:S(2)}) copy-start(bf16[1024,1024]{1,0:T(8,128)(2,1)} %param.28) | copy-start | bytes 6291460
  7.2 8.0 copy-start.51
  7.2 8.2 copy-start.44
  7.2 45.3 %all-gather.5.cloned.1.call-start = ((), (), s32[]{:S(2)}) async-start(), calls=%async_computation.8 | async-start | bytes 5242880 | tf_op jit(solution)/shard_map/all_gather | solution.py:164
  8.8 7.4 copy-start.31
  11.8 4.5 copy-start.27
  15.1 169.1 %reduce-scatter.5.cloned.1.call-start = ((), (), s32[]{:S(2)}) async-start(), calls=%async_computation.9 | async-start | bytes 5242880 | tf_op jit(solution)/shard_map/reduce_scatter | solution.py:191
  16.1 36.4 %copy-start.34 = (s32[2,6]{0,1:T(8,128)}, s32[2,6]{0,1:T(8,128)S(1)}, u32[]{:S(2)}) copy-start(s32[2,6]{0,1:T(8,128)S(1)} %reduce_window_sum.11) | copy-start | bytes 148
  16.3 36.2 %copy-start.29 = (s32[2,2048]{1,0:T(2,128)}, s32[2,2048]{1,0:T(2,128)S(1)}, u32[]{:S(2)}) copy-start(s32[2,2048]{1,0:T(2,128)S(1)} %fusion.165) | copy-start | bytes 49156
  75.1 4.4 copy-start.8
  75.1 4.4 copy-start.17
  90.8 4.4 copy-start.8
  90.8 4.4 copy-start.17
  106.5 4.4 copy-start.8
  106.5 4.4 copy-start.17
  122.2 4.4 copy-start.8
  139.6 106.2 %all-gather.7.cloned.1.call-start = ((), (), s32[]{:S(2)}) async-start(), calls=%async_computation.10 | async-start | bytes 5242880 | tf_op jit(solution)/shard_map/all_gather | solution.py:203
  139.7 50.4 %copy-start.50 = (s32[2,1,6]{2,1,0:T(1,128)S(1)}, s32[2,1,6]{2,1,0:T(1,128)}, u32[]{:S(2)}) copy-start(s32[2,1,6]{2,1,0:T(1,128)} %param.23) | copy-start | bytes 148
  139.7 50.5 %copy-start.45 = (s32[2,1,6]{2,1,0:T(1,128)S(1)}, s32[2,1,6]{2,1,0:T(1,128)}, u32[]{:S(2)}) copy-start(s32[2,1,6]{2,1,0:T(1,128)} %param.22) | copy-start | bytes 148
  139.7 50.9 %copy-start.35 = (s32[2,6]{0,1:T(8,128)S(1)}, s32[2,6]{0,1:T(8,128)}, u32[]{:S(2)}) copy-start(s32[2,6]{0,1:T(8,128)} %copy-done.34) | copy-start | bytes 148
  139.7 50.9 %copy-start.37 = (s32[2,6]{0,1:T(8,128)S(1)}, s32[2,6]{0,1:T(8,128)}, u32[]{:S(2)}) copy-start(s32[2,6]{0,1:T(8,128)} %copy-done.36) | copy-start | bytes 148
  139.7 50.9 %copy-start.30 = (s32[2,2048]{1,0:T(2,128)S(1)}, s32[2,2048]{1,0:T(2,128)}, u32[]{:S(2)}) copy-start(s32[2,2048]{1,0:T(2,128)} %copy-done.29) | copy-start | bytes 49156
  191.5 7.9 copy-start.42
  205.4 30.0 %all-to-all-start.2 = ((bf16[8,2,32768]{2,1,0:T(2,128)(2,1)}), bf16[8,2,32768]{2,1,0:T(2,128)(2,1)}, u32[]{:S(2)}, u32[]{:S(2)}) async-start(bf16[8,2,32768]{2,1,0:T(2,128)(2,1)} %reshape.982), calls=%async_computation.4 | async-start | bytes 2097152 | tf_op jit(solution)/shard_map/all_to_all | solution.py:232
  209.6 69.8 %all-gather.9.cloned.1.call-start = ((), (), s32[]{:S(2)}) async-start(), calls=%async_computation.12 | async-start | bytes 5242880 | tf_op jit(solution)/shard_map/all_gather | solution.py:250
  212.9 32.9 %copy-start.55 = (bf16[1024]{0:T(1024)(128)(2,1)S(1)}, bf16[1024]{0:T(1024)(128)(2,1)}, u32[]{:S(2)}) copy-start(bf16[1024]{0:T(1024)(128)(2,1)} %param.29) | copy-start | bytes 6148
  245.7 100.4 %reduce-scatter.9.cloned.1.call-start = ((), (), s32[]{:S(2)}) async-start(), calls=%async_computation.13 | async-start | bytes 5242880 | tf_op jit(solution)/shard_map/reduce_scatter | solution.py:262
  301.4 91.6 %reduce-scatter.7.cloned.1.call-start = ((), (), s32[]{:S(2)}) async-start(), calls=%async_computation.11 | async-start | bytes 5242880 | tf_op jit(solution)/shard_map/reduce_scatter | solution.py:210
  311.5 34.6 %copy-start.4 = (bf16[1,512,1,1024]{3,1,2,0:T(8,128)(2,1)S(1)}, bf16[1,512,1,1024]{3,1,2,0:T(8,128)(2,1)}, u32[]{:S(2)}) copy-start(bf16[1,512,1,1024]{3,1,2,0:T(8,128)(2,1)} %param.21) | copy-start | bytes 3145732
  311.5 34.6 %copy-start.7 = (bf16[512,1,1024]{2,0,1:T(8,128)(2,1)S(1)}, bf16[512,1,1024]{2,0,1:T(8,128)(2,1)}, u32[]{:S(2)}) copy-start(bf16[512,1,1024]{2,0,1:T(8,128)(2,1)} %reduce-scatter.5.cloned.1.call-done) | copy-start | bytes 3145732
  311.5 124.0 %all-gather.11.cloned.1.call-start = ((), (), s32[]{:S(2)}) async-start(), calls=%async_computation.14 | async-start | bytes 5242880 | tf_op jit(solution)/shard_map/all_gather | solution.py:275
  393.0 4.6 copy-start.12
  393.0 4.6 copy-start.13
  400.9 561.7 %all-reduce.5.cloned.1.call-start = ((), (), s32[]{:S(2)}) async-start(), calls=%async_computation.16 | async-start | bytes 12582912 | tf_op jit(solution)/shard_map/psum | solution.py:337
  400.9 9.5 copy-start.59
  400.9 9.5 copy-start.65
  410.4 25.1 %copy-start.63 = (bf16[256,1024]{1,0:T(8,128)(2,1)S(1)}, bf16[256,1024]{1,0:T(8,128)(2,1)}, u32[]{:S(2)}) copy-start(bf16[256,1024]{1,0:T(8,128)(2,1)} %param.26) | copy-start | bytes 1572868
  439.0 7.0 copy-start.9
  451.2 6.8 copy-start.2
  520.3 8.1 copy-start.2
  591.3 8.1 copy-start.2
  662.3 8.1 copy-start.2
  738.6 4.4 copy-start.21
  738.6 4.4 copy-start.24
  738.6 4.4 copy-start.26
  738.6 4.4 copy-start.58
  747.8 260.8 %reduce-scatter.11.cloned.1.call-start = ((), (), s32[]{:S(2)}) async-start(), calls=%async_computation.15 | async-start | bytes 5242880 | tf_op jit(solution)/shard_map/reduce_scatter | solution.py:312
  764.1 8.5 copy-start.5
  768.0 20.3 %all-to-all-start.3 = ((bf16[8,2,32768]{2,1,0:T(2,128)(2,1)}), bf16[8,2,32768]{2,1,0:T(2,128)(2,1)}, u32[]{:S(2)}, u32[]{:S(2)}) async-start(bf16[8,2,32768]{2,1,0:T(2,128)(2,1)} %reshape.988), calls=%async_computation.7 | async-start | bytes 2097152 | tf_op jit(solution)/shard_map/all_to_all | solution.py:239
  776.5 16.0 %copy-start.16 = (bf16[512,1,1024]{2,0,1:T(8,128)(2,1)S(1)}, bf16[512,1,1024]{2,0,1:T(8,128)(2,1)}, u32[]{:S(2)}) copy-start(bf16[512,1,1024]{2,0,1:T(8,128)(2,1)} %get-tuple-element.365) | copy-start | bytes 3145732
  788.3 22.3 %all-to-all-start.1 = ((bf16[8,2,32768]{2,1,0:T(2,128)(2,1)}), bf16[8,2,32768]{2,1,0:T(2,128)(2,1)}, u32[]{:S(2)}, u32[]{:S(2)}) async-start(bf16[8,2,32768]{2,1,0:T(2,128)(2,1)} %reshape.986), calls=%async_computation.3 | async-start | bytes 2097152 | tf_op jit(solution)/shard_map/all_to_all | solution.py:223
  796.5 17.9 %copy-start.33 = (s32[2,2048]{1,0:T(2,128)S(1)}, s32[2,2048]{1,0:T(2,128)}, u32[]{:S(2)}) copy-start(s32[2,2048]{1,0:T(2,128)} %get-tuple-element.373) | copy-start | bytes 49156
  810.6 31.1 %all-to-all-start = ((bf16[8,2,32768]{2,1,0:T(2,128)(2,1)}), bf16[8,2,32768]{2,1,0:T(2,128)(2,1)S(1)}, u32[]{:S(2)}, u32[]{:S(2)}) async-start(bf16[8,2,32768]{2,1,0:T(2,128)(2,1)} %reshape.984), calls=%async_computation.2 | async-start | bytes 2097152 | tf_op jit(solution)/shard_map/all_to_all | solution.py:222
  962.6 5.6 copy-start.20
  970.7 37.9 %copy-start.28 = (f32[1024]{0:T(1024)S(1)}, f32[1024]{0:T(1024)}, u32[]{:S(2)}) copy-start(f32[1024]{0:T(1024)} %copy-done.27) | copy-start | bytes 12292
  970.7 37.9 %copy-start.32 = (f32[512]{0:T(512)S(1)}, f32[512]{0:T(512)}, u32[]{:S(2)}) copy-start(f32[512]{0:T(512)} %copy-done.31) | copy-start | bytes 6148
  970.7 39.7 %copy-start.41 = (f32[512]{0:T(512)S(1)}, f32[512]{0:T(512)}, u32[]{:S(2)}) copy-start(f32[512]{0:T(512)} %copy-done.40) | copy-start | bytes 6148
  970.7 41.1 %copy-start.39 = (f32[512]{0:T(512)S(1)}, f32[512]{0:T(512)}, u32[]{:S(2)}) copy-start(f32[512]{0:T(512)} %copy-done.38) | copy-start | bytes 6148
  973.6 40.6 %copy-start.46 = (bf16[1024]{0:T(1024)(128)(2,1)S(1)}, bf16[1024]{0:T(1024)(128)(2,1)}, u32[]{:S(2)}) copy-start(bf16[1024]{0:T(1024)(128)(2,1)} %get-tuple-element.288) | copy-start | bytes 6148
  973.6 40.6 %copy-start.47 = (bf16[1024]{0:T(1024)(128)(2,1)S(1)}, bf16[1024]{0:T(1024)(128)(2,1)}, u32[]{:S(2)}) copy-start(bf16[1024]{0:T(1024)(128)(2,1)} %get-tuple-element.352) | copy-start | bytes 6148
  973.6 40.6 %copy-start.48 = (bf16[1024]{0:T(1024)(128)(2,1)S(1)}, bf16[1024]{0:T(1024)(128)(2,1)}, u32[]{:S(2)}) copy-start(bf16[1024]{0:T(1024)(128)(2,1)} %get-tuple-element.354) | copy-start | bytes 6148
  973.6 40.6 %copy-start.49 = (bf16[1024]{0:T(1024)(128)(2,1)S(1)}, bf16[1024]{0:T(1024)(128)(2,1)}, u32[]{:S(2)}) copy-start(bf16[1024]{0:T(1024)(128)(2,1)} %get-tuple-element.366) | copy-start | bytes 6148
  973.6 40.6 %copy-start.57 = (bf16[1024]{0:T(1024)(128)(2,1)S(1)}, bf16[1024]{0:T(1024)(128)(2,1)}, u32[]{:S(2)}) copy-start(bf16[1024]{0:T(1024)(128)(2,1)} %get-tuple-element.370) | copy-start | bytes 6148
  1052.3 18.2 %copy-start.1 = (bf16[1024,1024]{1,0:T(8,128)(2,1)S(1)}, bf16[1024,1024]{1,0:T(8,128)(2,1)}, u32[]{:S(2)}) copy-start(bf16[1024,1024]{1,0:T(8,128)(2,1)} %param.28) | copy-start | bytes 6291460
  (30 other events, 70.8 us)
Sparse Core Ops, SparseCore 0:
  15.3 37.1 all-gather.4
  139.7 44.4 reduce-scatter.4
  190.2 44.9 all-gather.6
  245.8 33.5 all-gather.8
  301.5 44.5 reduce-scatter.8
  348.5 44.4 reduce-scatter.6
  401.0 34.4 all-gather.10
  747.9 214.6 all-reduce.4
  965.1 43.4 reduce-scatter.10
where the time goes:
time: 1090 us; the launch traced here: 1080 us
  matrix products  445 us (41%)
  waiting for transfers between devices  351 us (32%)
  other arithmetic  104 us (10%)
  local copies, waits for them, and re-layouts  95.7 us (9%)
  blocking collectives  48.4 us (4%)
  starting transfers between devices  17.2 us (2%)
  between operations  14.8 us (1%)
    psum x1, waiting for transfers between devices, per_device(): lax.psum(grad_w_qkv_part.astype(jnp.bfloat16), ('section', 'rows'))  104 us
    dot_general x4, matrix products, one_block(): jnp.einsum('hqk,qhd->khd', grad_score, queries, preferred_element_type=jn...  104 us
    dot_general x4, matrix products, one_block(): jnp.einsum('hqk,khd->qhd', grad_score, key_seq, preferred_element_type=jn...  96 us
    unnamed x136, local copies, waits for them, and re-layouts  51.9 us
    reduce_scatter x1, waiting for transfers between devices, per_device(): lax.psum_scatter(jnp.einsum('rsf,fd->rsd', picked, w_down, preferred_elem...  44.9 us
    reduce_scatter x1, waiting for transfers between devices, per_device(): lax.psum_scatter(jnp.einsum('rsk,kd->rsd', picked, w_out, preferred_eleme...  44.5 us
    psum x1, blocking collectives, per_device(): lax.psum(grad_b_out.astype(jnp.bfloat16), ('section', 'rows'))  37.5 us
    all_gather x1, waiting for transfers between devices, per_device(): gathered_one = lax.all_gather(normed_one, 'heads', axis=0, tiled=True)  35 us
  transfers between devices with their start and end apart: 13, of which 10 were waited for; matrix products, arithmetic and copies ran while one was open for 17% of the time, Pallas kernels for 0%

commit v1 on v0

v1 whole, which is shorter than its diff:
```python
from functools import partial

import jax
import jax.numpy as jnp
from jax import lax
from jax.experimental import pallas as pl
from jax.experimental.pallas import tpu as pltpu
from jax.sharding import PartitionSpec as P

HD = 64
EPSILON = 1e-06
MASKED = -1e30
F32 = jnp.float32
BF = jnp.bfloat16
BQ = 128
BK = 256
LANE = 128
SLOT_XOR = (0, 2, 1, 3)


def nt(a,b): return lax.dot_general(a,b,(((1,),(1,)),((),())),preferred_element_type=F32)
def nn(a,b): return lax.dot_general(a,b,(((1,),(0,)),((),())),preferred_element_type=F32)

def stack_heads(rows, groups, hd):
    lane=lax.broadcasted_iota(jnp.int32, rows.shape, 1)//hd
    zero=jnp.zeros_like(rows)
    return jnp.concatenate([jnp.where(lane==g, rows, zero) for g in range(groups)], axis=0)

def diag_t(acc, groups, hd, bq):
    return jnp.concatenate([acc[g*hd:(g+1)*hd, g*bq:(g+1)*bq] for g in range(groups)], axis=0)

def key_off(slot_ref, kb):
    per=512//BK
    return pl.multiple_of(slot_ref[kb//per]*512 + lax.rem(kb,per)*BK, BK)

def fwd_kernel(groups, hd, lo_ref, hi_ref, slot_ref, q_ref, k_ref, v_ref, sq_ref, sk_ref, o_ref, lse_ref, vt_ref, acc_ref):
    i=pl.program_id(0)
    @pl.when(i==0)
    def _():
        for b in range(v_ref.shape[0]//BK):
            vt_ref[:, b*BK:(b+1)*BK]=jnp.transpose(v_ref[b*BK:(b+1)*BK,:].astype(F32)).astype(BF)
    q4=stack_heads(q_ref[...]*jnp.asarray(hd**-0.5,BF), groups, hd)
    acc_ref[...]=jnp.zeros_like(acc_ref)
    segq=sq_ref[...][0]
    pairs=groups//2
    def step(kb, carry):
        off=key_off(slot_ref,kb)
        kblk=k_ref[pl.ds(off,BK),:]
        mask=sk_ref[pl.ds(off,BK),:]==segq
        mask=jnp.concatenate([mask]*2,axis=1)
        out=[]
        ss=[nt(kblk, q4[g*2*BQ:(g+1)*2*BQ]) for g in range(pairs)]
        for g in range(pairs):
            m,l=carry[g]
            s=jnp.where(mask,ss[g],MASKED)
            m2=jnp.maximum(m,jnp.max(s,axis=0,keepdims=True))
            p=jnp.exp(s-m2)
            a=jnp.exp(m-m2)
            l=l*a+jnp.sum(p,axis=0,keepdims=True)
            pv=nn(vt_ref[g*2*hd:(g+1)*2*hd,pl.ds(off,BK)], p.astype(BF))
            for e in range(2):
                r=slice((2*g+e)*hd,(2*g+e+1)*hd)
                acc_ref[r,:]=acc_ref[r,:]*a[:,e*BQ:(e+1)*BQ]+pv[e*hd:(e+1)*hd,e*BQ:(e+1)*BQ]
            out.append((m2,l))
        return tuple(out)
    init=tuple((jnp.full((1,2*BQ),-jnp.inf,F32),jnp.zeros((1,2*BQ),F32)) for _ in range(pairs))
    res=lax.fori_loop(lo_ref[i],hi_ref[i],step,init)
    m=jnp.concatenate([r[0] for r in res],axis=1)
    l=jnp.concatenate([r[1] for r in res],axis=1)
    inv=1.0/l
    for h in range(groups):
        acc_ref[h*hd:(h+1)*hd,:]*=inv[:,h*BQ:(h+1)*BQ]
    o_ref[...]=jnp.transpose(acc_ref[...]).astype(BF)
    lse_ref[...]=(m+jnp.log(l))[None]

def bwd_kernel(groups, hd, lo_ref, hi_ref, slot_ref, q_ref, k_ref, v_ref, sq_ref, sk_ref, o_ref, lse_ref, do_ref,
               dq_ref, dk_ref, dv_ref, kt_ref, acc_ref, dka_ref, dva_ref):
    i=pl.program_id(0)
    @pl.when(i==0)
    def _():
        for b in range(k_ref.shape[0]//BK):
            kt_ref[:, b*BK:(b+1)*BK]=jnp.transpose(k_ref[b*BK:(b+1)*BK,:].astype(F32)).astype(BF)
        dka_ref[...]=jnp.zeros_like(dka_ref)
        dva_ref[...]=jnp.zeros_like(dva_ref)
    scale=jnp.asarray(hd**-0.5,BF)
    q4=stack_heads(q_ref[...]*scale, groups, hd)
    do=do_ref[...]
    d4=stack_heads(do, groups, hd)
    prod=jnp.transpose(do.astype(F32)*o_ref[...].astype(F32))
    delta=jnp.concatenate([jnp.sum(prod[g*hd:(g+1)*hd],axis=0,keepdims=True) for g in range(groups)],axis=1)
    lse=lse_ref[...][0]
    acc_ref[...]=jnp.zeros_like(acc_ref)
    segq=sq_ref[...][0]
    pairs=groups//2
    w=2*BQ
    def step(kb, carry):
        off=key_off(slot_ref,kb)
        rows=pl.ds(off,BK)
        kblk=k_ref[rows,:]; vblk=v_ref[rows,:]
        mask=sk_ref[rows,:]==segq
        mask=jnp.concatenate([mask]*2,axis=1)
        ss=[(nt(kblk, q4[g*w:(g+1)*w]),nt(vblk, d4[g*w:(g+1)*w])) for g in range(pairs)]
        ps=[];dss=[]
        for g in range(pairs):
            s,dp=ss[g]
            p=jnp.exp(jnp.where(mask,s,MASKED)-lse[:,g*w:(g+1)*w])
            ds=(p*(dp-delta[:,g*w:(g+1)*w])).astype(BF)
            ps.append(p.astype(BF)); dss.append(ds)
            dq=nn(kt_ref[g*2*hd:(g+1)*2*hd,rows], ds)
            for e in range(2):
                r=slice((2*g+e)*hd,(2*g+e+1)*hd)
                acc_ref[r,:]+=dq[e*hd:(e+1)*hd,e*BQ:(e+1)*BQ]
        dva_ref[rows,:]+=nn(jnp.concatenate(ps,axis=1), d4)
        dka_ref[rows,:]+=nn(jnp.concatenate(dss,axis=1), q4)
        return carry
    lax.fori_loop(lo_ref[i],hi_ref[i],step,0)
    dq_ref[...]=(jnp.transpose(acc_ref[...])*(hd**-0.5)).astype(BF)
    @pl.when(i==pl.num_programs(0)-1)
    def _():
        dk_ref[...]=dka_ref[...].astype(BF)
        dv_ref[...]=dva_ref[...].astype(BF)

def _specs(L,W,groups):
    blk=pl.BlockSpec((BQ,W),lambda i,*_:(i,0))
    full=pl.BlockSpec((L,W),lambda i,*_:(0,0))
    sq=pl.BlockSpec((1,1,BQ),lambda i,*_:(i,0,0))
    sk=pl.BlockSpec((L,BQ),lambda i,*_:(0,0))
    st=pl.BlockSpec((1,1,groups*BQ),lambda i,*_:(i,0,0))
    return blk,full,sq,sk,st

def attend_fwd(q,k,v,sq,sk,lo,hi,slot,hd=64):
    L,W=q.shape; groups=W//hd; n=L//BQ
    blk,full,sqs,sks,st=_specs(L,W,groups)
    return pl.pallas_call(partial(fwd_kernel,groups,hd),
      grid_spec=pltpu.PrefetchScalarGridSpec(num_scalar_prefetch=3,grid=(n,),
        in_specs=[blk,full,full,sqs,sks],out_specs=[blk,st],
        scratch_shapes=[pltpu.VMEM((W,L),BF),pltpu.VMEM((W,BQ),F32)]),
      out_shape=[jax.ShapeDtypeStruct((L,W),BF),jax.ShapeDtypeStruct((n,1,groups*BQ),F32)],
      compiler_params=pltpu.CompilerParams(vmem_limit_bytes=32<<20),
      cost_estimate=pl.CostEstimate(flops=8*10**9,transcendentals=5*10**6,bytes_accessed=5<<20),
      name="attend_fwd")(lo,hi,slot,q,k,v,sq,sk)

def attend_bwd(q,k,v,sq,sk,lo,hi,slot,o,lse,do,hd=64):
    L,W=q.shape; groups=W//hd; n=L//BQ
    blk,full,sqs,sks,st=_specs(L,W,groups)
    return pl.pallas_call(partial(bwd_kernel,groups,hd),
      grid_spec=pltpu.PrefetchScalarGridSpec(num_scalar_prefetch=3,grid=(n,),
        in_specs=[blk,full,full,sqs,sks,blk,st,blk],out_specs=[blk,full,full],
        scratch_shapes=[pltpu.VMEM((W,L),BF),pltpu.VMEM((W,BQ),F32),pltpu.VMEM((L,W),F32),pltpu.VMEM((L,W),F32)]),
      out_shape=[jax.ShapeDtypeStruct((L,W),BF)]*3,
      compiler_params=pltpu.CompilerParams(vmem_limit_bytes=40<<20),
      cost_estimate=pl.CostEstimate(flops=20*10**9,transcendentals=5*10**6,bytes_accessed=8<<20),
      name="attend_bwd")(lo,hi,slot,q,k,v,sq,sk,o,lse,do)


def const_spec(shape):
    zeros = (0,) * len(shape)
    return pl.BlockSpec(shape, lambda *_: zeros, pipeline_mode=pl.Buffered(1))


def norm_parts(rows):
    average = jnp.mean(rows, axis=-1, keepdims=True)
    centred = rows - average
    inverse = lax.rsqrt(jnp.mean(centred * centred, axis=-1, keepdims=True) + EPSILON)
    return centred * inverse, inverse


def norm_back(cotangent, normed, inverse):
    first = jnp.mean(cotangent, axis=-1, keepdims=True)
    second = jnp.mean(cotangent * normed, axis=-1, keepdims=True)
    return (cotangent - first - normed * second) * inverse


def column_block(me_ref, e):
    return pl.multiple_of(jnp.bitwise_xor(me_ref[0], e) * LANE, LANE)


def enter_kernel(with_norm, me_ref, t_ref, gain_ref, shift_ref, w_ref, bq_ref, bv_ref, *outs):
    if with_norm:
        h_ref, tap_ref, q_ref, k_ref, v_ref = outs
        normed, _ = norm_parts(t_ref[...].astype(F32))
        h = (normed * gain_ref[...] + shift_ref[...]).astype(BF)
        h_ref[...] = h
        for n, e in enumerate((0, 1, 4, 5)):
            tap_ref[n] = t_ref[:, pl.ds(column_block(me_ref, e), LANE)]
    else:
        q_ref, k_ref, v_ref = outs
        h = t_ref[...]
    q_ref[...] = (nn(h, w_ref[0]) + bq_ref[...]).astype(BF)
    k_ref[...] = nn(h, w_ref[1]).astype(BF)
    v_ref[...] = (nn(h, w_ref[2]) + bv_ref[...]).astype(BF)


def enter(rows, me8, gain, shift, w3, bq, bv, with_norm):
    count, width = rows.shape
    part = w3.shape[2]
    step = min(256, count)
    row = lambda w: pl.BlockSpec((step, w), lambda i, *_: (i, 0))
    outs = [(row(part), jax.ShapeDtypeStruct((count, part), BF))] * 3
    if with_norm:
        outs = [
            (row(width), jax.ShapeDtypeStruct((count, width), BF)),
            (pl.BlockSpec((4, step, LANE), lambda i, *_: (0, i, 0)), jax.ShapeDtypeStruct((4, count, LANE), BF)),
        ] + outs
    return pl.pallas_call(
        partial(enter_kernel, with_norm),
        grid_spec=pltpu.PrefetchScalarGridSpec(
            num_scalar_prefetch=1,
            grid=(count // step,),
            in_specs=[row(width), const_spec((1, width)), const_spec((1, width)), const_spec(w3.shape),
                      const_spec((1, part)), const_spec((1, part))],
            out_specs=[o[0] for o in outs],
        ),
        out_shape=[o[1] for o in outs],
        compiler_params=pltpu.CompilerParams(vmem_limit_bytes=32 << 20),
        cost_estimate=pl.CostEstimate(flops=6 * count * width * part, transcendentals=0, bytes_accessed=6 * count * width),
        name="enter_norm" if with_norm else "enter_plain",
    )(me8, rows, gain, shift, w3, bq, bv)


def reorder_kernel(sources, natural_out, arrays, starts_ref, shifts_ref, out_pos_ref, in_pos_ref, half_ref, *refs):
    ins, outs = refs[: -arrays - 2], refs[-arrays - 2 : -2]
    buf, val = refs[-2:]
    for j in range(2):
        half = jnp.bitwise_xor(half_ref[0], j)
        for a in range(arrays):
            for t, n in enumerate(sources[j][a]):
                rows = ins[n][half] if len(ins[n].shape) == 3 else ins[n][...]
                where_to = pl.ds(pl.multiple_of(in_pos_ref[t] + BQ, BQ), rows.shape[0])
                buf[a, where_to, :] = rows.astype(F32)

        def one_block(i, carry):
            base = out_pos_ref[i]
            place = base + lax.broadcasted_iota(jnp.int32, (BQ, LANE), 0)
            for piece in range(7):
                low = starts_ref[half, piece]
                high = starts_ref[half, piece + 1]

                @pl.when((low < base + BQ) & (high > base))
                def _():
                    keep = (place >= low) & (place < high)
                    for a in range(arrays):
                        rows = buf[a, pl.ds(base + shifts_ref[half, piece] + BQ, BQ), :]
                        val[a] = jnp.where(keep, rows, val[a])

            where_to = pl.ds(pl.multiple_of(i * BQ, BQ), BQ)
            for a in range(arrays):
                outs[a][half if natural_out else j, where_to, :] = val[a].astype(BF)
            return carry

        lax.fori_loop(0, out_pos_ref.shape[0], one_block, 0)


def reorder(operands, sources, natural_out, table, out_pos, in_pos, half, name):
    length = out_pos.shape[0] * BQ
    arrays = len(sources[0])
    return pl.pallas_call(
        partial(reorder_kernel, sources, natural_out, arrays),
        grid_spec=pltpu.PrefetchScalarGridSpec(
            num_scalar_prefetch=5,
            grid=(1,),
            in_specs=[const_spec(o.shape) for o in operands],
            out_specs=[const_spec((2, length, LANE))] * arrays,
            scratch_shapes=[pltpu.VMEM((arrays, length + 2 * BQ, LANE), F32), pltpu.VMEM((arrays, BQ, LANE), F32)],
        ),
        out_shape=[jax.ShapeDtypeStruct((2, length, LANE), BF)] * arrays,
        compiler_params=pltpu.CompilerParams(vmem_limit_bytes=32 << 20),
        cost_estimate=pl.CostEstimate(flops=10**6, transcendentals=0, bytes_accessed=arrays * length * 4 * LANE * 2),
        name=name,
    )(*table, out_pos, in_pos, half, *operands)


TAIL_P = 0.28
TAIL_C = (0.1165205699350068, 0.06749810405563278, 0.2689066993976019, -0.23698906730009697, 0.3898712275439997, -0.10580754284907957)


def erf_tail(x):
    bell = jnp.exp(-0.5 * x * x)
    t = 1.0 / (1.0 + TAIL_P * jnp.abs(x))
    poly = jnp.full_like(t, TAIL_C[-1])
    for c in TAIL_C[-2::-1]:
        poly = poly * t + c
    return poly * t * bell, bell * 0.3989422804014327


def gelu_pair(u):
    tail, density = erf_tail(u)
    cdf = jnp.where(u >= 0.0, 1.0 - tail, tail)
    return u * cdf, cdf + u * density


def assemble(scratch_ref, local_ref, remote_ref, me_ref):
    for n, e in enumerate((0, 1, 4, 5)):
        scratch_ref[e] = local_ref[n]
        scratch_ref[e ^ 2] = remote_ref[n]
    return jnp.concatenate([scratch_ref[jnp.bitwise_xor(me_ref[0], j)] for j in range(8)], axis=1)


def middle_kernel(alias, chunk, me_ref, pos_ref, t_ref, o0, o1, o2, o3, gl_ref, gr_ref, w0, w1, w2, w3, bo_ref, g_ref, b_ref,
                  up0, up1, bu0, bu1, dn0, dn1, bd_ref, *rest):
    rest = rest[alias:]
    x1_ref, h2_ref, gz_ref, a0, a1, d0, d1, dh_ref, zm_ref, zs_ref, db_ref, gs_ref, z_ref = rest
    i = pl.program_id(0)
    attn = nn(o0[...], w0[...]) + nn(o1[...], w1[...]) + nn(o2[...], w2[...]) + nn(o3[...], w3[...])
    x1 = t_ref[...].astype(F32) + (attn + bo_ref[...])
    x1_ref[...] = x1
    normed, _ = norm_parts(x1)
    h2 = (normed * g_ref[...] + b_ref[...]).astype(BF)
    h2_ref[...] = h2
    gz = assemble(gs_ref, gl_ref, gr_ref, me_ref)
    place = pos_ref[i] + lax.broadcasted_iota(jnp.int32, gz.shape, 0)
    gz = jnp.where(place < pos_ref[pos_ref.shape[0] - 1], gz, jnp.zeros_like(gz))
    gz_ref[...] = gz

    @pl.when(i == 0)
    def _():
        db_ref[...] = jnp.zeros_like(db_ref)

    z = x1 + bd_ref[...]
    dh = None
    for half, (up, bu, dn, a, d) in enumerate(((up0, bu0, dn0, a0, d0), (up1, bu1, dn1, a1, d1))):
        for c in range(0, up.shape[1], chunk):
            cols = slice(c, c + chunk)
            u = nn(h2, up[:, cols]) + bu[:, cols]
            back = nt(gz, dn[cols, :])
            act, slope = gelu_pair(u)
            act = act.astype(BF)
            grad = back * slope
            a[:, cols] = act
            du = grad.astype(BF)
            d[:, cols] = du
            db_ref[half : half + 1, cols] += jnp.sum(du.astype(F32), axis=0, keepdims=True)
            if half == 0 and c == 0:
                zp = nn(act, dn[cols, :])
                dh = nt(du, up[:, cols])
            else:
                zp = zp + nn(act, dn[cols, :])
                dh = dh + nt(du, up[:, cols])
    dh_ref[...] = dh.astype(dh_ref.dtype)
    z_ref[0] = z + zp
    z_ref[1] = zp
    for n, e in enumerate((0, 1, 4, 5)):
        zm_ref[n] = z_ref[0, :, pl.ds(column_block(me_ref, e), LANE)]
        zs_ref[n] = z_ref[1, :, pl.ds(column_block(me_ref, e ^ 2), LANE)].astype(BF)


def middle(me8, pos, which, tokens, outs4, g_loc, g_rem, wo4, b_out, gain, shift, ups, bups, downs, b_down, held, dh_type):
    count, width = tokens.shape
    step = min(256, count)
    grid = count // step
    hidden = ups[0].shape[1]
    part = outs4[0].shape[1]
    first = which * grid
    row = lambda w: pl.BlockSpec((step, w), lambda i, *_: (i, 0))
    row_at = lambda w: pl.BlockSpec((step, w), lambda i, *_: (first + i, 0))
    four = pl.BlockSpec((4, step, LANE), lambda i, *_: (0, i, 0))
    four_at = pl.BlockSpec((4, step, LANE), lambda i, *_: (0, first + i, 0))
    in_specs = (
        [row(width)] + [row_at(part)] * 2 + [row(part)] * 2 + [four_at, four]
        + [const_spec((part, width))] * 4 + [const_spec((1, width))] * 3
        + [const_spec((width, hidden))] * 2 + [const_spec((1, hidden))] * 2 + [const_spec((hidden, width))] * 2
        + [const_spec((1, width))]
    )
    operands = [tokens, *outs4, g_loc, g_rem, *wo4, b_out, gain, shift, *ups, *bups, *downs, b_down]
    total = 2 * count
    shared = [(total, width)] * 2 + [(total, hidden)] * 4
    out_shape = (
        [jax.ShapeDtypeStruct((count, width), F32)] + [jax.ShapeDtypeStruct(s, BF) for s in shared]
        + [jax.ShapeDtypeStruct((count, width), dh_type), jax.ShapeDtypeStruct((4, count, LANE), F32),
           jax.ShapeDtypeStruct((4, count, LANE), BF), jax.ShapeDtypeStruct((8, hidden), F32)]
    )
    out_specs = (
        [row(width)] + [row_at(s[1]) for s in shared]
        + [row(width), four, four, pl.BlockSpec((8, hidden), lambda i, *_: (0, 0))]
    )
    aliases = {}
    if held is not None:
        for n, h in enumerate(held):
            aliases[2 + len(operands)] = 1 + n
            operands.append(h)
            in_specs.append(pl.BlockSpec(memory_space=pl.ANY))
    return pl.pallas_call(
        partial(middle_kernel, len(aliases), 512),
        grid_spec=pltpu.PrefetchScalarGridSpec(
            num_scalar_prefetch=2,
            grid=(grid,),
            in_specs=in_specs,
            out_specs=out_specs,
            scratch_shapes=[pltpu.VMEM((8, step, LANE), BF), pltpu.VMEM((2, step, width), F32)],
        ),
        out_shape=out_shape,
        input_output_aliases=aliases,
        compiler_params=pltpu.CompilerParams(vmem_limit_bytes=56 << 20),
        cost_estimate=pl.CostEstimate(flops=18 * count * width * hidden, transcendentals=4 * count * hidden, bytes_accessed=30 << 20),
        name="middle_own" if which == 0 else "middle_partner",
    )(me8, pos, *operands)


def second_kernel(dh_ref, dr_ref, x1_ref, gz_ref, g_ref, w0, w1, w2, w3, dx_ref, ga_ref, do0, do1, dox, sum_ref):
    dh = dh_ref[...] + dr_ref[...].astype(F32)
    normed, inverse = norm_parts(x1_ref[...])
    gz = gz_ref[...].astype(F32)
    dx = norm_back(dh * g_ref[...], normed, inverse) + gz
    dx_ref[...] = dx
    ga = dx.astype(BF)
    ga_ref[...] = ga
    part = w0.shape[0]
    do0[...] = nt(ga, w0[...]).astype(BF)
    do1[...] = nt(ga, w1[...]).astype(BF)
    dox[:, :part] = nt(ga, w2[...]).astype(BF)
    dox[:, part:] = nt(ga, w3[...]).astype(BF)

    @pl.when(pl.program_id(0) == 0)
    def _():
        sum_ref[...] = jnp.zeros_like(sum_ref)

    for n, v in enumerate((dh * normed, dh, ga.astype(F32), gz)):
        sum_ref[n : n + 1, :] += jnp.sum(v, axis=0, keepdims=True)


def second(dh, dr, x1, gz, gain, wo4):
    count, width = dh.shape
    part = wo4[0].shape[0]
    step = min(256, count)
    row = lambda w: pl.BlockSpec((step, w), lambda i: (i, 0))
    return pl.pallas_call(
        second_kernel,
        grid=(count // step,),
        in_specs=[row(width)] * 4 + [const_spec((1, width))] + [const_spec((part, width))] * 4,
        out_specs=[row(width), row(width), row(part), row(part), row(2 * part), pl.BlockSpec((8, width), lambda i: (0, 0))],
        out_shape=[jax.ShapeDtypeStruct((count, width), F32), jax.ShapeDtypeStruct((count, width), BF),
                   jax.ShapeDtypeStruct((count, part), BF), jax.ShapeDtypeStruct((count, part), BF),
                   jax.ShapeDtypeStruct((count, 2 * part), BF), jax.ShapeDtypeStruct((8, width), F32)],
        compiler_params=pltpu.CompilerParams(vmem_limit_bytes=32 << 20),
        cost_estimate=pl.CostEstimate(flops=8 * count * width * part, transcendentals=0, bytes_accessed=14 * count * width),
        name="second_norm_back",
    )(dh, dr, x1, gz, gain, *wo4)


def first_kernel(me_ref, dh_ref, dr_ref, t_ref, dx_ref, gl_ref, gr_ref, g_ref, out_ref, sum_ref, gs_ref):
    dh = dh_ref[...] + dr_ref[...].astype(F32)
    normed, inverse = norm_parts(t_ref[...].astype(F32))
    tap = assemble(gs_ref, gl_ref, gr_ref, me_ref).astype(F32)
    out_ref[...] = norm_back(dh * g_ref[...], normed, inverse) + dx_ref[...] + tap

    @pl.when(pl.program_id(0) == 0)
    def _():
        sum_ref[...] = jnp.zeros_like(sum_ref)

    for n, v in enumerate((dh * normed, dh)):
        sum_ref[n : n + 1, :] += jnp.sum(v, axis=0, keepdims=True)


def first(me8, dh, dr, tokens, dx, tap_loc, tap_rem, gain):
    count, width = dh.shape
    step = min(256, count)
    row = pl.BlockSpec((step, width), lambda i, *_: (i, 0))
    four = pl.BlockSpec((4, step, LANE), lambda i, *_: (0, i, 0))
    return pl.pallas_call(
        first_kernel,
        grid_spec=pltpu.PrefetchScalarGridSpec(
            num_scalar_prefetch=1,
            grid=(count // step,),
            in_specs=[row] * 4 + [four, four, const_spec((1, width))],
            out_specs=[row, pl.BlockSpec((8, width), lambda i, *_: (0, 0))],
            scratch_shapes=[pltpu.VMEM((8, step, LANE), BF)],
        ),
        out_shape=[jax.ShapeDtypeStruct((count, width), F32), jax.ShapeDtypeStruct((8, width), F32)],
        compiler_params=pltpu.CompilerParams(vmem_limit_bytes=32 << 20),
        cost_estimate=pl.CostEstimate(flops=20 * count * width, transcendentals=0, bytes_accessed=16 * count * width),
        name="first_norm_back",
    )(me8, dh, dr, tokens, dx, tap_loc, tap_rem, gain)


def tn(a, b):
    return lax.dot_general(a, b, (((0,), (0,)), ((), ())), preferred_element_type=F32)


def lookup(table, index):
    hit = index[:, None] == jnp.arange(table.shape[0], dtype=jnp.int32)[None, :]
    return jnp.sum(jnp.where(hit, table[None, :], 0), axis=1).astype(jnp.int32)


def running(values):
    count = values.shape[-1]
    upto = jnp.arange(count)[:, None] <= jnp.arange(count)[None, :]
    return jnp.sum(jnp.where(upto, values[..., :, None], 0), axis=-2).astype(jnp.int32)


def order_tables(lengths, ranks, length):
    ends = running(lengths)
    begins = ends - lengths
    earlier = ranks[:, None, :] < ranks[:, :, None]
    moved = jnp.sum(jnp.where(earlier, lengths[:, None, :], 0), axis=2).astype(jnp.int32)
    at_rank = ranks[:, None, :] == jnp.arange(ranks.shape[1], dtype=jnp.int32)[None, :, None]
    by_rank = lambda v: jnp.sum(jnp.where(at_rank, v[:, None, :], 0), axis=2).astype(jnp.int32)
    tail = ends[:, -1:]
    stop = jnp.full_like(tail, length)
    zero = jnp.zeros_like(tail)
    source = (jnp.concatenate([by_rank(moved), tail, stop], axis=1), jnp.concatenate([by_rank(begins - moved), zero], axis=1))
    target = (jnp.concatenate([begins, tail, stop], axis=1), jnp.concatenate([moved - begins, zero], axis=1))
    return ends, source, target


def per_device(tokens, image_lengths, tile_ranks, w_qkv, bias_qv, w_out, bias_out, w_up, bias_up, w_down, bias_down,
               ln1_gain, ln1_bias, ln2_gain, ln2_bias, grad_out, grad_tap):
    own = tokens[0, :, 0, :]
    rows, width = own.shape
    length = 4 * rows
    part = w_out.shape[0]
    section_at = lax.axis_index("section").astype(jnp.int32)
    head_at = lax.axis_index("heads").astype(jnp.int32)
    pair = lambda v: lax.ppermute(v, "heads", [(0, 2), (2, 0), (1, 3), (3, 1)])
    sibling = lambda v: lax.ppermute(v, "heads", [(0, 1), (1, 0), (2, 3), (3, 2)])
    across = lambda v: lax.ppermute(v, "section", [(0, 1), (1, 0)])
    as_row = lambda v: v.astype(F32).reshape(1, -1)
    me8 = (section_at * 4 + head_at).reshape(1)
    half_at = section_at.reshape(1)

    ends_all, source, target = order_tables(image_lengths[:, 0, :], tile_ranks[:, 0, :], length)
    ends = lax.dynamic_index_in_dim(ends_all, section_at, 0, keepdims=False)
    xors = jnp.array(SLOT_XOR, jnp.int32)
    slot_block = jnp.bitwise_xor(head_at, xors)
    slot = lookup(xors, jnp.bitwise_xor(jnp.arange(4, dtype=jnp.int32), head_at))
    slot_pos = slot_block * rows
    row_pos = (slot_pos[:, None] + jnp.arange(rows, dtype=jnp.int32)[None, :]).reshape(-1)
    block_pos = (slot_pos[:, None] + jnp.arange(0, rows, BQ, dtype=jnp.int32)[None, :]).reshape(-1)
    segment = jnp.sum((row_pos[:, None] >= ends[None, :]).astype(jnp.int32), axis=1)
    begins_pad = jnp.concatenate([jnp.zeros((1,), jnp.int32), ends])
    ends_pad = jnp.concatenate([ends, jnp.full((1,), length, jnp.int32)])
    seg_first = jnp.sum((block_pos[:, None] >= ends[None, :]).astype(jnp.int32), axis=1)
    seg_last = jnp.sum((block_pos[:, None] + (BQ - 1) >= ends[None, :]).astype(jnp.int32), axis=1)
    low = lookup(begins_pad, seg_first) // BK
    high = (lookup(ends_pad, seg_last) + BK - 1) // BK
    seg_q = segment.reshape(-1, 1, BQ)
    seg_k = jnp.broadcast_to(segment[:, None], (length, BQ))
    total = ends[-1:]
    valid = (row_pos < total).astype(F32)

    partner = pair(own)
    ups = (w_up, sibling(w_up))
    downs = (w_down, sibling(w_down))
    bups = (as_row(bias_up), as_row(sibling(bias_up)))
    wo_partner = pair(w_out)
    wo4 = (w_out, sibling(w_out), wo_partner, sibling(wo_partner))
    w3 = jnp.transpose(w_qkv, (1, 0, 2))
    w3_sib = sibling(w3)

    back_out, back_tap = reorder([grad_out[:, :, 0, :], grad_tap[:, :, 0, :]], (((0,), (1,)),) * 2, False, target, block_pos,
                                 jnp.zeros((1,), jnp.int32), half_at, "reorder_back")
    both = jnp.stack([back_out[0], back_tap[0], across(back_out[1]), across(back_tap[1])])
    from_sib = sibling(both[:, 2 * rows :])
    g_loc = jnp.stack([both[0, : 2 * rows], from_sib[0], both[2, : 2 * rows], from_sib[2]])
    t_loc = jnp.stack([both[1, : 2 * rows], from_sib[1], both[3, : 2 * rows], from_sib[3]])
    g_rem_own = pair(g_loc[:, rows:])
    g_rem_partner = pair(g_loc[:, :rows])
    t_rem = pair(t_loc[:, rows:])

    gain1, shift1 = as_row(ln1_gain), as_row(ln1_bias)
    bq, bv = as_row(bias_qv[0]), as_row(bias_qv[1])
    h_own, tap_own, q0, k0, v0 = enter(own, me8, gain1, shift1, w3, bq, bv, True)
    h_partner, tap_partner, q1, k1, v1 = enter(partner, me8, gain1, shift1, w3, bq, bv, True)
    h_sib = sibling(h_own)
    h_sib_partner = sibling(h_partner)
    q2, k2, v2 = enter(h_sib, me8, gain1, shift1, w3, bq, bv, False)
    q3, k3, v3 = enter(h_sib_partner, me8, gain1, shift1, w3, bq, bv, False)
    query = jnp.concatenate([q0, q1, q2, q3])
    key = jnp.concatenate([k0, k1, k2, k3])
    value = jnp.concatenate([v0, v1, v2, v3])
    mixed, log_sum = attend_fwd(query, key, value, seg_q, seg_k, low, high, slot)

    def to_decoder(four_own, four_partner):
        keep = jnp.concatenate([four_own, four_partner], axis=1)
        got = sibling(keep[1::2])
        mine = jnp.concatenate([keep[0::2], got], axis=1)
        return mine[0], across(mine[1])

    tap_mine, tap_other = to_decoder(tap_own, tap_partner)

    mixed_sib = sibling(mixed[2 * rows :])
    mixed_loc = jnp.concatenate([mixed[: 2 * rows], mixed_sib], axis=1)
    rem_partner = pair(mixed_loc[:rows])
    rem_own = pair(mixed_loc[rows:])

    gain2, shift2 = as_row(ln2_gain), as_row(ln2_bias)
    b_out, b_down = as_row(bias_out), as_row(bias_down)
    step = min(256, rows)
    pos_of = lambda b: jnp.concatenate([slot_pos[b] + jnp.arange(0, rows, step, dtype=jnp.int32), total])

    def run_middle(which, toks, rem, g_rem, held, dh_type):
        outs4 = (mixed, mixed_sib, rem[:, :part], rem[:, part:])
        return middle(me8, pos_of(which), which, toks, outs4, g_loc, g_rem, wo4, b_out, gain2, shift2,
                      ups, bups, downs, b_down, held, dh_type)

    done1 = run_middle(1, partner, rem_partner, g_rem_partner, None, BF)
    dh_send = done1[7]
    dh_recv = pair(dh_send)
    z_recv1 = pair(done1[9])
    done0 = run_middle(0, own, rem_own, g_rem_own, list(done1[1:7]), F32)
    z_recv0 = pair(done0[9])
    x1_own = done0[0]
    h2, gz, act0, act1, du0, du1 = done0[1:7]
    dh_own = done0[7]
    mask4 = valid[: 2 * rows].reshape(1, 2 * rows, 1)
    y_own = ((done0[8] + z_recv1.astype(F32)) * mask4[:, :rows]).astype(BF)
    y_partner = ((done1[8] + z_recv0.astype(F32)) * mask4[:, rows:]).astype(BF)
    out_mine, out_other = to_decoder(y_own, y_partner)

    natural_blocks = jnp.arange(0, length, BQ, dtype=jnp.int32)

    def slots(v):
        return [v[t * rows : (t + 1) * rows] for t in range(4)]

    four = lambda n: tuple(range(4 * n, 4 * n + 4))
    output_dec, tap_dec = reorder(
        slots(out_mine) + slots(tap_mine) + slots(out_other) + slots(tap_other), ((four(0), four(1)), (four(2), four(3))),
        True, source, natural_blocks, slot_pos, half_at, "reorder_out",
    )

    down_own = tn(act0, gz)
    down_sib = sibling(tn(act1, gz).astype(BF))
    up_own = tn(h2, du0)
    up_sib = sibling(tn(h2, du1).astype(BF))
    grad_down = (down_own + down_sib.astype(F32)).astype(BF)
    grad_up = (up_own + up_sib.astype(F32)).astype(BF)
    grad_down, grad_up = lax.psum((grad_down, grad_up), ("section", "rows"))
    bias_up_part = done0[10][:2] + done1[10][:2]

    dx1, ga, do_own, do_sib, do_x, sums2 = second(dh_own, dh_recv, x1_own, gz[:rows], gain2, wo4)
    do_r = pair(do_x)
    do_for_sib = jnp.concatenate([do_sib, do_r[:, part:]])
    do_from_sib = sibling(do_for_sib)
    grad_mixed = jnp.concatenate([do_own, do_r[:, :part], do_from_sib])
    dq, dk, dv = attend_bwd(query, key, value, seg_q, seg_k, low, high, slot, mixed, log_sum, grad_mixed)

    wo_mine = tn(jnp.concatenate([mixed[:rows], rem_own[:, :part]], axis=1), ga)
    wo_theirs = tn(jnp.concatenate([mixed_sib[:rows], rem_own[:, part:]], axis=1), ga)
    wo_sum = wo_mine + sibling(wo_theirs.astype(BF)).astype(F32)
    grad_wo = wo_sum[:part] + pair(wo_sum[part:].astype(BF)).astype(F32)

    d3 = jnp.stack([dq, dk, dv])
    d3_sib = sibling(d3[:, 2 * rows :])

    def project_back(lo):
        total_back = None
        for n in range(3):
            for piece, weight in ((d3[n, lo : lo + rows], w3[n]), (d3_sib[n, lo : lo + rows], w3_sib[n])):
                term = nt(piece, weight)
                total_back = term if total_back is None else total_back + term
        return total_back

    dh1_recv = pair(project_back(rows).astype(BF))
    dh1_own = project_back(0)
    h_all = jnp.concatenate([h_own, h_partner, h_sib, h_sib_partner])
    grad_w3 = jnp.stack([tn(h_all, dq), tn(h_all, dk), tn(h_all, dv)])
    grad_wo, grad_w3 = lax.psum((grad_wo.astype(BF), grad_w3.astype(BF)), ("section", "rows"))
    grad_tokens, sums1 = first(me8, dh1_own, dh1_recv, own, dx1, t_loc[:, :rows], t_rem, gain1)

    bias_up_own = bias_up_part[0] + sibling(bias_up_part[1])
    bqv = jnp.concatenate([jnp.sum(dq.astype(F32), axis=0), jnp.sum(dv.astype(F32), axis=0)])
    small = lax.psum(jnp.concatenate([sums1[:2], sums2[:4]]), ("section", "rows", "heads"))
    mine = lax.psum(jnp.concatenate([bias_up_own, bqv]), ("section", "rows"))
    hidden = bias_up_own.shape[0]
    return (
        output_dec[:, :, None, :],
        tap_dec[:, :, None, :],
        grad_tokens[None, :, None, :],
        jnp.transpose(grad_w3, (1, 0, 2)).astype(F32),
        mine[hidden:].reshape(2, part),
        grad_wo.astype(F32),
        small[4],
        grad_up.astype(F32),
        mine[:hidden],
        grad_down.astype(F32),
        small[5],
        small[0],
        small[1],
        small[2],
        small[3],
    )


def solution(mesh):
    placed = (
        P("section", "heads", "rows", None),
        P(None, "rows", None),
        P(None, "rows", None),
        P(None, None, "heads"),
        P(None, "heads"),
        P("heads", None),
        P(),
        P(None, "heads"),
        P("heads"),
        P("heads", None),
        P(),
        P(),
        P(),
        P(),
        P(),
        P(None, None, "rows", ("section", "heads")),
        P(None, None, "rows", ("section", "heads")),
    )
    return jax.shard_map(
        per_device,
        mesh=mesh,
        in_specs=placed,
        out_specs=(
            P(None, None, "rows", ("section", "heads")),
            P(None, None, "rows", ("section", "heads")),
            P("section", "heads", "rows", None),
            P(None, None, "heads"),
            P(None, "heads"),
            P("heads", None),
            P(),
            P(None, "heads"),
            P("heads"),
            P("heads", None),
            P(),
            P(),
            P(),
            P(),
            P(),
        ),
        check_vma=False,
    )
```

time: 1090 us -> 532 us (0.49)
  matrix products: 445 us -> 45.4 us
  waiting for transfers between devices: 351 us -> 172 us
  Pallas kernels: 0 us -> 134 us
  other arithmetic: 104 us -> 32 us
  local copies, waits for them, and re-layouts: 95.7 us -> 38.5 us
  blocking collectives: 48.4 us -> 63.7 us
    dot_general x44 -> x21, matrix products: 445 us -> 45.4 us  [the longest x9 24.2 us: tn(): lax.dot_general(a, b, (((0,), (0,)), ((), ())), preferred_element_type=F32)]
    reduce_scatter x4 -> x0, waiting for transfers between devices: 158 us -> none  [the longest x1 44.9 us: per_device(): lax.psum_scatter(jnp.einsum('rsf,fd->rsd', picked, w_down, preferred_elem...]
    pallas_call x0 -> x12, Pallas kernels: none -> 134 us  [the longest x2 45.4 us: middle(): pl.pallas_call(partial(middle_kernel, len(aliases), 512), grid_spec=pltpu...]
    ppermute x0 -> x35, waiting for transfers between devices: none -> 94.1 us  [the longest x13 71.2 us: per_device(): pair = lambda v: lax.ppermute(v, 'heads', [(0, 2), (2, 0), (1, 3), (3, 1)])]
    all_gather x4 -> x0, waiting for transfers between devices: 61.9 us -> none  [the longest x1 35 us: per_device(): gathered_one = lax.all_gather(normed_one, 'heads', axis=0, tiled=True)]
    reduce_sum x20 -> x9, other arithmetic: 45.6 us -> 1.64 us  [the longest x1 0.29 us: per_device(): jnp.sum(dv.astype(F32), axis=0)]
    unnamed x136 -> x192, local copies, waits for them, and re-layouts: 51.9 us -> 19.9 us
    all_to_all x4 -> x0, waiting for transfers between devices: 27 us -> none  [the longest x1 22.5 us: per_device(): lax.all_to_all(back_out.reshape(encoder_shape), ('section', 'heads'), spl...]
  transfers between devices with their start and end apart: 13 -> 36, of which waited for: 10 -> 10; matrix products, arithmetic and copies ran while one was open for 17% -> 18% of each run, Pallas kernels for 0% -> 26%
where the time goes in v1:
time: 532 us; the launch traced here: 524 us
  waiting for transfers between devices  172 us (32%)
  Pallas kernels  134 us (25%)
  blocking collectives  63.7 us (12%)
  matrix products  45.4 us (9%)
  local copies, waits for them, and re-layouts  38.5 us (7%)
  other arithmetic  32 us (6%)
  starting transfers between devices  23.1 us (4%)
  between operations  15.7 us (3%)
    psum x1, waiting for transfers between devices, per_device(): lax.psum((grad_wo.astype(BF), grad_w3.astype(BF)), ('section', 'rows'))  77.9 us
    ppermute x13, waiting for transfers between devices, per_device(): pair = lambda v: lax.ppermute(v, 'heads', [(0, 2), (2, 0), (1, 3), (3, 1)])  71.2 us
    pallas_call x2, Pallas kernels, middle(): pl.pallas_call(partial(middle_kernel, len(aliases), 512), grid_spec=pltpu...  45.4 us
    psum x1, blocking collectives, per_device(): lax.psum(jnp.concatenate([sums1[:2], sums2[:4]]), ('section', 'rows', 'he...  39.5 us
    pallas_call x1, Pallas kernels, attend_bwd(): pl.pallas_call(partial(bwd_kernel, groups, hd), grid_spec=pltpu.PrefetchS...  32.7 us
    pallas_call x1, Pallas kernels, attend_fwd(): pl.pallas_call(partial(fwd_kernel, groups, hd), grid_spec=pltpu.PrefetchS...  26.4 us
    dot_general x9, matrix products, tn(): lax.dot_general(a, b, (((0,), (0,)), ((), ())), preferred_element_type=F32)  24.2 us
    psum x1, blocking collectives, per_device(): mine = lax.psum(jnp.concatenate([bias_up_own, bqv]), ('section', 'rows'))  24.2 us
  transfers between devices with their start and end apart: 36, of which 10 were waited for; matrix products, arithmetic and copies ran while one was open for 18% of the time, Pallas kernels for 26%

profile of v1, /device:TPU:0, one launch (start us, length us, event | category | flops | bytes accessed | tf_op | source)
XLA Modules:
  0.0 524.2 jit_solution(3615371063483745830)
XLA Ops:
  7.3 3.0 collective-permute-start
  13.6 3.8 enter_norm.2
  22.8 3.9 reorder_back.1
  27.7 1.5 collective-permute-start.6
  38.9 2.3 constant_dynamic-update-slice_fusion.17
  41.8 1.2 pad_add_fusion.pos_ref
  48.3 5.3 %collective-permute-done.5 = bf16[2048,128]{1,0:T(8,128)(2,1)} collective-permute-done((bf16[2048,128]{1,0:T(8,128)(2,1)}, bf16[2048,128]{1,0:T(8,128)(2,1)}, u32[]{:S(2)}, u32[]{:S(2)}) %collective-permute-start.5) | collective-permute-done | bytes 524320 | tf_op jit(solution)/shard_map/ppermute | solution.py:515
  56.1 1.3 pad_maximum_fusion.2
  57.5 3.6 enter_norm.3
  61.8 3.1 enter_plain.2
  65.2 1.3 constant_dynamic-update-slice_fusion.15
  66.7 2.6 enter_plain.3
  69.8 26.4 %attend_fwd.1 = (bf16[2048,256]{1,0:T(8,128)(2,1)S(1)}, f32[16,1,512]{2,1,0:T(1,128)S(1)}) custom-call(s32[16]{0:T(128)S(1)} %and_select_fusion.1.lo_ref, s32[16]{0:T(128)S(1)} %and_select_fusion.hi_ref, s32[4]{0:T(128)S(1)} %select_reduce_fusion.5.slot_ref, bf16[2048,256]{1,0:T(8,128)(2,1)S(1)} %constant_dynamic-update-slice_fusion.q_ref, ...), custom_call_target="tpu_custom_call" | custom-call | flops 8000000000 | bytes 5242880 | tf_op jit(solution)/shard_map/attend_fwd/pallas_call | solution.py:134
  101.5 12.1 %collective-permute-done.15 = bf16[512,512]{1,0:T(8,128)(2,1)S(1)} collective-permute-done((bf16[512,512]{1,0:T(8,128)(2,1)S(1)}, bf16[512,512]{1,0:T(8,128)(2,1)S(1)}, u32[]{:S(2)}, u32[]{:S(2)}) %collective-permute-start.15) | collective-permute-done | bytes 524320 | tf_op jit(solution)/shard_map/ppermute | solution.py:513
  115.6 1.8 collective-permute-start.8
  117.4 11.0 %collective-permute-done.16.gr_ref = bf16[4,512,128]{2,1,0:T(8,128)(2,1)S(1)} collective-permute-done((bf16[4,512,128]{2,1,0:T(8,128)(2,1)S(1)}, bf16[4,512,128]{2,1,0:T(8,128)(2,1)S(1)}, u32[]{:S(2)}, u32[]{:S(2)}) %collective-permute-start.16) | collective-permute-done | bytes 524320 | tf_op jit(solution)/shard_map/ppermute | solution.py:513
  128.4 2.0 collective-permute-start.22
  131.8 1.3 copy-done.78
  133.1 22.8 %middle_partner.1 = (f32[512,1024]{1,0:T(8,128)}, bf16[1024,1024]{1,0:T(8,128)(2,1)}, bf16[1024,1024]{1,0:T(8,128)(2,1)}, bf16[1024,1024]{1,0:T(8,128)(2,1)}, bf...) custom-call(s32[1]{0:T(128)} %bitcast.7.me_ref, ...), custom_call_target="tpu_custom_call" | custom-call | flops 9663676416 | bytes 31457280 | tf_op jit(solution)/shard_map/middle_partner/pallas_call | solution.py:382
  158.3 22.6 %middle_own.1 = (f32[512,1024]{1,0:T(8,128)}, bf16[1024,1024]{1,0:T(8,128)(2,1)}, bf16[1024,1024]{1,0:T(8,128)(2,1)}, bf16[1024,1024]{1,0:T(8,128)(2,1)}, bf16[1...) custom-call(s32[1]{0:T(128)} %bitcast.7.me_ref, ...), custom_call_target="tpu_custom_call", output_to_operand_aliasing={{1}: (23, {}), {2}: (24, {}), {3}: (25, {}), {4}: (26, {}),... | custom-call | flops 9663676416 | bytes 31457280 | tf_op jit(solution)/shard_map/middle_own/pallas_call | solution.py:382
  180.9 4.8 convolution_convert_fusion
  186.8 1.3 collective-permute-start.18
  188.8 3.8 convolution_convert_fusion.1
  192.6 1.4 slice_add_fusion.1
  194.1 4.0 second_norm_back.1
  198.2 3.4 collective-permute-done.18
  201.6 1.3 collective-permute-start.24
  203.2 9.7 %collective-permute-done.17 = bf16[4,512,128]{2,1,0:T(8,128)(2,1)S(1)} collective-permute-done((bf16[4,512,128]{2,1,0:T(8,128)(2,1)S(1)}, bf16[4,512,128]{2,1,0:T(8,128)(2,1)S(1)}, u32[]{:S(2)}, u32[]{:S(2)}) %collective-permute-start.17) | collective-permute-done | bytes 524320 | tf_op jit(solution)/shard_map/ppermute | solution.py:513
  213.2 6.6 %collective-permute-done.24 = bf16[512,512]{1,0:T(8,128)(2,1)S(1)} collective-permute-done((bf16[512,512]{1,0:T(8,128)(2,1)S(1)}, bf16[512,512]{1,0:T(8,128)(2,1)S(1)}, u32[]{:S(2)}, u32[]{:S(2)}) %collective-permute-start.24) | collective-permute-done | bytes 524320 | tf_op jit(solution)/shard_map/ppermute | solution.py:513
  221.1 1.7 convolution_convert_fusion.2
  223.6 32.7 %attend_bwd.1 = (bf16[2048,256]{1,0:T(8,128)(2,1)S(1)}, bf16[2048,256]{1,0:T(8,128)(2,1)S(1)}, bf16[2048,256]{1,0:T(8,128)(2,1)S(1)}) custom-call(s32[16]{0:T(128)S(1)} %copy-done.44, s32[16]{0:T(128)S(1)} %copy-done.46, s32[4]{0:T(128)S(1)} %copy-done.42, bf16[2048,256]{1,0:T(8,128)(2,1)S(1)} %copy-done.34, bf16[2048,256]{1,0:T(8,128)(2,1)S(1)} %copy-done.31, ...), custom_call_target="tpu_custom_call" | custom-call | flops 20000000000 | bytes 8388608 | tf_op jit(solution)/shard_map/attend_bwd/pallas_call | solution.py:146
  256.3 1.3 fusion.2
  257.6 1.3 fusion.1
  258.9 1.3 fusion
  260.3 1.4 maximum_bitcast_fusion
  261.7 1.5 collective-permute-start.29
  264.2 5.5 %add_convert_fusion.1 = bf16[1024,1024]{1,0:T(8,128)(2,1)} fusion(bf16[1024,1024]{1,0:T(8,128)(2,1)} %collective-permute-done.33, bf16[1024,1024]{1,0:T(8,128)(2,1)S(1)} %copy-done.85, bf16[1024,1024]{1,0:T(8,128)(2,1)S(1)} %copy-done.87), kind=kOutput, calls=%fused_computation.1 | convolution fusion | flops 2150629376 | bytes 8388608 | tf_op jit(solution)/shard_map/dot_general | solution.py:476
  270.9 3.8 add_convert_fusion
  274.7 12.8 %collective-permute-done.32 = bf16[256,1024]{1,0:T(8,128)(2,1)S(1)} collective-permute-done((bf16[256,1024]{1,0:T(8,128)(2,1)S(1)}, bf16[256,1024]{1,0:T(8,128)(2,1)S(1)}, u32[]{:S(2)}, u32[]{:S(2)}) %collective-permute-start.32) | collective-permute-done | bytes 524320 | tf_op jit(solution)/shard_map/ppermute | solution.py:513
  294.2 17.6 %collective-permute-done.21 = bf16[2048,128]{1,0:T(8,128)(2,1)S(1)} collective-permute-done((bf16[2048,128]{1,0:T(8,128)(2,1)S(1)}, bf16[2048,128]{1,0:T(8,128)(2,1)S(1)}, u32[]{:S(2)}, u32[]{:S(2)}) %collective-permute-start.21) | collective-permute-done | bytes 524320 | tf_op jit(solution)/shard_map/ppermute | solution.py:515
  311.8 5.2 reorder_out.1
  317.1 1.3 pad_maximum_fusion
  318.9 2.8 fusion.22
  321.8 24.2 %psum.43 = f32[1536]{0:T(1024)S(1)} all-reduce(f32[1536]{0:T(1024)S(1)} %pad_maximum_fusion.14), channel_id=1, replica_groups=mesh['section'=2,'rows'=4,'heads'=4] {'section','rows'}, use_global_device_ids=true, to_apply=%region_13.14 | all-reduce | flops 1536 | bytes 12288 | tf_op jit(solution)/shard_map/psum | solution.py:662
  347.1 1.5 fusion.18
  348.7 1.5 fusion.14
  350.2 1.5 fusion.21
  351.7 1.5 fusion.17
  353.2 1.5 fusion.13
  354.8 1.6 fusion.19
  356.3 1.6 fusion.15
  357.9 2.0 add_convert_fusion.2
  360.0 1.7 collective-permute-start.28
  361.7 1.6 fusion.20
  363.3 1.7 fusion.16
  365.1 2.2 add_add_fusion.dh_ref
  367.3 15.6 %collective-permute-done.28.dr_ref = bf16[512,1024]{1,0:T(8,128)(2,1)S(1)} collective-permute-done((bf16[512,1024]{1,0:T(8,128)(2,1)S(1)}, bf16[512,1024]{1,0:T(8,128)(2,1)S(1)}, u32[]{:S(2)}, u32[]{:S(2)}) %collective-permute-start.28) | collective-permute-done | bytes 1048608 | tf_op jit(solution)/shard_map/ppermute | solution.py:513
  382.9 3.1 first_norm_back.1
  386.1 3.5 copy.57
  389.6 39.5 %psum.45 = f32[6,1024]{1,0:T(8,128)S(1)} all-reduce(f32[6,1024]{1,0:T(8,128)S(1)} %pad_maximum_fusion.13), channel_id=1, replica_groups=mesh['section'=2,'rows'=4,'heads'=4] {'section','rows','heads'}, use_global_device_ids=true, to_apply=%region_15.16 | all-reduce | flops 6144 | bytes 49152 | tf_op jit(solution)/shard_map/psum | solution.py:661
  429.7 77.9 %all-reduce.5.cloned.1.call-done = (bf16[1024,3,256]{2,0,1:T(8,128)(2,1)}, bf16[256,1024]{1,0:T(8,128)(2,1)}, bf16[1024,1024]{1,0:T(8,128)(2,1)}, bf16[1024,1024]{1,0:T(8,128)(2,1)}) async-done(((bf16[1024,3,256]{2,0,1:T(8,128)(2,1)}, bf16[256,1024]{1,0:T(8,128)(2,1)}, bf16[1024,1024]{1,0:T(8,128)(2,1)}, bf16[1024,1024]{1,0:T(8,128)(2,1)}), (bf16[1024,3,256]{2,0,1:T(8,128)(2,1)}, ...) | async-done | bytes 6291472 | tf_op jit(solution)/shard_map/psum | solution.py:656
  507.6 3.5 convert_element_type.105
  512.2 2.5 convert_element_type.116
  514.7 2.5 convert_element_type.120
  (349 shorter events, 56.9 us)
Async XLA Ops:
  7.2 13.5 %copy-start.83 = (s32[4]{0:T(128)S(1)}, s32[4]{0:T(128)}, u32[]{:S(2)}) copy-start(s32[4]{0:T(128)} %constant.65.clone) | copy-start | bytes 52
  7.2 12.4 %copy-start.69 = (s32[2,1,6]{2,1,0:T(1,128)S(1)}, s32[2,1,6]{2,1,0:T(1,128)}, u32[]{:S(2)}) copy-start(s32[2,1,6]{2,1,0:T(1,128)} %param.20) | copy-start | bytes 148
  7.2 12.5 %copy-start.68 = (s32[2,1,6]{2,1,0:T(1,128)S(1)}, s32[2,1,6]{2,1,0:T(1,128)}, u32[]{:S(2)}) copy-start(s32[2,1,6]{2,1,0:T(1,128)} %param.19) | copy-start | bytes 148
  7.2 500.4 %all-reduce.5.cloned.1.call-start = ((), (), s32[]{:S(2)}) async-start(), calls=%async_computation | async-start | bytes 12582912 | tf_op jit(solution)/shard_map/psum | solution.py:656
  7.3 50.2 %collective-permute-start = (bf16[512,1024]{1,0:T(8,128)(2,1)}, bf16[512,1024]{1,0:T(8,128)(2,1)}, u32[]{:S(2)}, u32[]{:S(2)}) collective-permute-start(bf16[512,1024]{1,0:T(8,128)(2,1)} %bitcast.179), channel_id=1, source_target_pairs={{0,2},{2,0},{1,3},{3,1},{4,6},{6,4},{5,7},{7,5},{8,10},{10,8},{9,1... | collective-permute-start | bytes 3145736 | tf_op jit(solution)/shard_map/ppermute | solution.py:513
  19.6 41.6 %collective-permute-start.1 = (bf16[512,1024]{1,0:T(8,128)(2,1)}, bf16[512,1024]{1,0:T(8,128)(2,1)}, u32[]{:S(2)}, u32[]{:S(2)}) collective-permute-start(bf16[512,1024]{1,0:T(8,128)(2,1)} %get-tuple-element.71), channel_id=1, source_target_pairs={{0,1},{1,0},{2,3},{3,2},{4,5},{5,4},{6,7},{7,6},{8,9},{9,8},{10,11... | collective-permute-start | bytes 3145736 | tf_op jit(solution)/shard_map/ppermute | solution.py:514
  27.7 26.9 %collective-permute-start.6 = (bf16[2048,128]{1,0:T(8,128)(2,1)}, bf16[2048,128]{1,0:T(8,128)(2,1)}, u32[]{:S(2)}, u32[]{:S(2)}) collective-permute-start(bf16[2048,128]{1,0:T(8,128)(2,1)} %get-tuple-element.195), channel_id=1, source_target_pairs={{0,16},{16,0},{1,17},{17,1},{2,18},{18,2},{3,19},{19,3},{4,20},{20... | collective-permute-start | bytes 1572872 | tf_op jit(solution)/shard_map/ppermute | solution.py:515
  30.3 23.3 %collective-permute-start.5 = (bf16[2048,128]{1,0:T(8,128)(2,1)}, bf16[2048,128]{1,0:T(8,128)(2,1)}, u32[]{:S(2)}, u32[]{:S(2)}) collective-permute-start(bf16[2048,128]{1,0:T(8,128)(2,1)} %get-tuple-element.193), channel_id=1, source_target_pairs={{0,16},{16,0},{1,17},{17,1},{2,18},{18,2},{3,19},{19,3},{4,20},{20... | collective-permute-start | bytes 1572872 | tf_op jit(solution)/shard_map/ppermute | solution.py:515
  30.8 16.6 %collective-permute-start.13 = (bf16[1024]{0:T(1024)(128)(2,1)S(1)}, bf16[1024]{0:T(1024)(128)(2,1)S(1)}, u32[]{:S(2)}, u32[]{:S(2)}) collective-permute-start(bf16[1024]{0:T(1024)(128)(2,1)S(1)} %copy-done.76), channel_id=1, source_target_pairs={{0,1},{1,0},{2,3},{3,2},{4,5},{5,4},{6,7},{7,6},{8,9},{9,8},{10,11... | collective-permute-start | bytes 6152 | tf_op jit(solution)/shard_map/ppermute | solution.py:514
  33.5 36.2 %copy-start.43 = (s32[16]{0:T(128)}, s32[16]{0:T(128)S(1)}, u32[]{:S(2)}) copy-start(s32[16]{0:T(128)S(1)} %and_select_fusion.1.lo_ref) | copy-start | bytes 196
  33.7 36.0 %copy-start.41 = (s32[4]{0:T(128)}, s32[4]{0:T(128)S(1)}, u32[]{:S(2)}) copy-start(s32[4]{0:T(128)S(1)} %select_reduce_fusion.5.slot_ref) | copy-start | bytes 52
  36.1 10.7 %copy-start.75 = (bf16[1024]{0:T(1024)(128)(2,1)S(1)}, bf16[1024]{0:T(1024)(128)(2,1)}, u32[]{:S(2)}) copy-start(bf16[1024]{0:T(1024)(128)(2,1)} %param.28) | copy-start | bytes 6148
  36.2 11.3 %copy-start.14 = (bf16[256,1024]{1,0:T(8,128)(2,1)S(1)}, bf16[256,1024]{1,0:T(8,128)(2,1)}, u32[]{:S(2)}) copy-start(bf16[256,1024]{1,0:T(8,128)(2,1)} %w0.5) | copy-start | bytes 1572868
  41.2 28.6 %copy-start.45 = (s32[16]{0:T(128)}, s32[16]{0:T(128)S(1)}, u32[]{:S(2)}) copy-start(s32[16]{0:T(128)S(1)} %and_select_fusion.hi_ref) | copy-start | bytes 196
  47.4 50.2 %collective-permute-start.10 = (bf16[256,1024]{1,0:T(8,128)(2,1)S(1)}, bf16[256,1024]{1,0:T(8,128)(2,1)S(1)}, u32[]{:S(2)}, u32[]{:S(2)}) collective-permute-start(bf16[256,1024]{1,0:T(8,128)(2,1)S(1)} %copy-done.14), channel_id=1, source_target_pairs={{0,2},{2,0},{1,3},{3,1},{4,6},{6,4},{5,7},{7,5},{8,10},{10,8},{9,1... | collective-permute-start | bytes 1572872 | tf_op jit(solution)/shard_map/ppermute | solution.py:513
  53.6 76.8 %collective-permute-start.12 = (bf16[1024,1024]{1,0:T(8,128)(2,1)}, bf16[1024,1024]{1,0:T(8,128)(2,1)S(1)}, u32[]{:S(2)}, u32[]{:S(2)}) collective-permute-start(bf16[1024,1024]{1,0:T(8,128)(2,1)} %up0.3), channel_id=1, source_target_pairs={{0,1},{1,0},{2,3},{3,2},{4,5},{5,4},{6,7},{7,6},{8,9},{9,8},{10,11... | collective-permute-start | bytes 6291464 | tf_op jit(solution)/shard_map/ppermute | solution.py:514
  54.6 76.4 %collective-permute-start.14 = (bf16[1024,1024]{1,0:T(8,128)(2,1)}, bf16[1024,1024]{1,0:T(8,128)(2,1)S(1)}, u32[]{:S(2)}, u32[]{:S(2)}) collective-permute-start(bf16[1024,1024]{1,0:T(8,128)(2,1)} %dn0.3), channel_id=1, source_target_pairs={{0,1},{1,0},{2,3},{3,2},{4,5},{5,4},{6,7},{7,6},{8,9},{9,8},{10,11... | collective-permute-start | bytes 6291464 | tf_op jit(solution)/shard_map/ppermute | solution.py:514
  57.4 38.9 %collective-permute-start.7 = (bf16[4,1024,128]{2,1,0:T(8,128)(2,1)S(1)}, bf16[4,1024,128]{2,1,0:T(8,128)(2,1)S(1)}, u32[]{:S(2)}, u32[]{:S(2)}) collective-permute-start(bf16[4,1024,128]{2,1,0:T(8,128)(2,1)S(1)} %pad_maximum_fusion.2), channel_id=1, source_target_pairs={{0,1},{1,0},{2,3},{3,2},{4,5},{5,4},{6,7},{7,6},{8,9},{9,8},{10,11... | collective-permute-start | bytes 3145736 | tf_op jit(solution)/shard_map/ppermute | solution.py:514
  61.2 5.3 %collective-permute-start.2 = (bf16[512,1024]{1,0:T(8,128)(2,1)S(1)}, bf16[512,1024]{1,0:T(8,128)(2,1)S(1)}, u32[]{:S(2)}, u32[]{:S(2)}) collective-permute-start(bf16[512,1024]{1,0:T(8,128)(2,1)S(1)} %get-tuple-element.73), channel_id=1, source_target_pairs={{0,1},{1,0},{2,3},{3,2},{4,5},{5,4},{6,7},{7,6},{8,9},{9,8},{10,11... | collective-permute-start | bytes 3145736 | tf_op jit(solution)/shard_map/ppermute | solution.py:514
  66.6 31.6 %collective-permute-start.20 = (bf16[2,1024,128]{2,1,0:T(8,128)(2,1)S(1)}, bf16[2,1024,128]{2,1,0:T(8,128)(2,1)S(1)}, u32[]{:S(2)}, u32[]{:S(2)}) collective-permute-start(bf16[2,1024,128]{2,1,0:T(8,128)(2,1)S(1)} %get-tuple-element.184), channel_id=1, source_target_pairs={{0,1},{1,0},{2,3},{3,2},{4,5},{5,4},{6,7},{7,6},{8,9},{9,8},{10,11... | collective-permute-start | bytes 1572872 | tf_op jit(solution)/shard_map/ppermute | solution.py:514
  69.3 26.8 %copy-start.33 = (bf16[2048,256]{1,0:T(8,128)(2,1)}, bf16[2048,256]{1,0:T(8,128)(2,1)S(1)}, u32[]{:S(2)}) copy-start(bf16[2048,256]{1,0:T(8,128)(2,1)S(1)} %constant_dynamic-update-slice_fusion.q_ref) | copy-start | bytes 3145732
  69.4 26.8 %copy-start.30 = (bf16[2048,256]{1,0:T(8,128)(2,1)}, bf16[2048,256]{1,0:T(8,128)(2,1)S(1)}, u32[]{:S(2)}) copy-start(bf16[2048,256]{1,0:T(8,128)(2,1)S(1)} %constant_dynamic-update-slice_fusion.4.k_ref) | copy-start | bytes 3145732
  69.4 26.8 %copy-start.27 = (bf16[2048,256]{1,0:T(8,128)(2,1)}, bf16[2048,256]{1,0:T(8,128)(2,1)S(1)}, u32[]{:S(2)}) copy-start(bf16[2048,256]{1,0:T(8,128)(2,1)S(1)} %constant_dynamic-update-slice_fusion.8.v_ref) | copy-start | bytes 3145732
  96.2 18.4 %copy-start.5 = (bf16[2048,256]{1,0:T(8,128)(2,1)}, bf16[2048,256]{1,0:T(8,128)(2,1)S(1)}, u32[]{:S(2)}) copy-start(bf16[2048,256]{1,0:T(8,128)(2,1)S(1)} %get-tuple-element.83.o0.o_ref) | copy-start | bytes 3145732
  96.3 2.9 collective-permute-start.3
  97.7 17.9 %collective-permute-start.9 = (bf16[256,1024]{1,0:T(8,128)(2,1)S(1)}, bf16[256,1024]{1,0:T(8,128)(2,1)S(1)}, u32[]{:S(2)}, u32[]{:S(2)}) collective-permute-start(bf16[256,1024]{1,0:T(8,128)(2,1)S(1)} %copy-done.14), channel_id=1, source_target_pairs={{0,1},{1,0},{2,3},{3,2},{4,5},{5,4},{6,7},{7,6},{8,9},{9,8},{10,11... | collective-permute-start | bytes 1572872 | tf_op jit(solution)/shard_map/ppermute | solution.py:514
  98.2 17.4 %collective-permute-start.11 = (bf16[256,1024]{1,0:T(8,128)(2,1)S(1)}, bf16[256,1024]{1,0:T(8,128)(2,1)S(1)}, u32[]{:S(2)}, u32[]{:S(2)}) collective-permute-start(bf16[256,1024]{1,0:T(8,128)(2,1)S(1)} %collective-permute-done.10.w2), channel_id=1, source_target_pairs={{0,1},{1,0},{2,3},{3,2},{4,5},{5,4},{6,7},{7,6},{8,9},{9,8},{10,11... | collective-permute-start | bytes 1572872 | tf_op jit(solution)/shard_map/ppermute | solution.py:514
  99.1 15.5 %copy-start.55 = (bf16[1024,256]{1,0:T(8,128)(2,1)}, bf16[1024,256]{1,0:T(8,128)(2,1)S(1)}, u32[]{:S(2)}) copy-start(bf16[1024,256]{1,0:T(8,128)(2,1)S(1)} %collective-permute-done.3.o1) | copy-start | bytes 1572868
  99.2 14.3 %collective-permute-start.15 = (bf16[512,512]{1,0:T(8,128)(2,1)S(1)}, bf16[512,512]{1,0:T(8,128)(2,1)S(1)}, u32[]{:S(2)}, u32[]{:S(2)}) collective-permute-start(bf16[512,512]{1,0:T(8,128)(2,1)S(1)} %get-tuple-element.191), channel_id=1, source_target_pairs={{0,2},{2,0},{1,3},{3,1},{4,6},{6,4},{5,7},{7,5},{8,10},{10,8},{9,1... | collective-permute-start | bytes 1572872 | tf_op jit(solution)/shard_map/ppermute | solution.py:513
  113.6 14.8 %collective-permute-start.16 = (bf16[4,512,128]{2,1,0:T(8,128)(2,1)S(1)}, bf16[4,512,128]{2,1,0:T(8,128)(2,1)S(1)}, u32[]{:S(2)}, u32[]{:S(2)}) collective-permute-start(bf16[4,512,128]{2,1,0:T(8,128)(2,1)S(1)} %get-tuple-element.189), channel_id=1, source_target_pairs={{0,2},{2,0},{1,3},{3,1},{4,6},{6,4},{5,7},{7,5},{8,10},{10,8},{9,1... | collective-permute-start | bytes 1572872 | tf_op jit(solution)/shard_map/ppermute | solution.py:513
  114.6 16.3 %copy-start.63 = (bf16[2048,1024]{1,0:T(8,128)(2,1)}, bf16[2048,1024]{1,0:T(8,128)(2,1)S(1)}, u32[]{:S(2)}) copy-start(bf16[2048,1024]{1,0:T(8,128)(2,1)S(1)} %constant_dynamic-update-slice_fusion.14) | copy-start | bytes 12582916
  115.6 17.5 %copy-start.18 = (bf16[256,1024]{1,0:T(8,128)(2,1)}, bf16[256,1024]{1,0:T(8,128)(2,1)S(1)}, u32[]{:S(2)}) copy-start(bf16[256,1024]{1,0:T(8,128)(2,1)S(1)} %collective-permute-done.9.w1) | copy-start | bytes 1572868
  115.6 239.2 %collective-permute-start.27 = (bf16[3,1024,256]{2,1,0:T(8,128)(2,1)}, bf16[3,1024,256]{2,1,0:T(8,128)(2,1)}, u32[]{:S(2)}, u32[]{:S(2)}) collective-permute-start(bf16[3,1024,256]{2,1,0:T(8,128)(2,1)} %bitcast.14.w_ref), channel_id=1, source_target_pairs={{0,1},{1,0},{2,3},{3,2},{4,5},{5,4},{6,7},{7,6},{8,9},{9,8},{10,11... | collective-permute-start | bytes 4718600 | tf_op jit(solution)/shard_map/ppermute | solution.py:514
  115.6 17.5 %copy-start.20 = (bf16[256,1024]{1,0:T(8,128)(2,1)}, bf16[256,1024]{1,0:T(8,128)(2,1)S(1)}, u32[]{:S(2)}) copy-start(bf16[256,1024]{1,0:T(8,128)(2,1)S(1)} %collective-permute-done.11.w3) | copy-start | bytes 1572868
  115.6 42.0 %collective-permute-start.8 = (bf16[4,512,128]{2,1,0:T(8,128)(2,1)}, bf16[4,512,128]{2,1,0:T(8,128)(2,1)S(1)}, u32[]{:S(2)}, u32[]{:S(2)}) collective-permute-start(bf16[4,512,128]{2,1,0:T(8,128)(2,1)} %get-tuple-element.188), channel_id=1, source_target_pairs={{0,2},{2,0},{1,3},{3,1},{4,6},{6,4},{5,7},{7,5},{8,10},{10,8},{9,1... | collective-permute-start | bytes 1572872 | tf_op jit(solution)/shard_map/ppermute | solution.py:513
  128.4 163.0 %collective-permute-start.22 = (bf16[2048,128]{1,0:T(8,128)(2,1)}, bf16[2048,128]{1,0:T(8,128)(2,1)}, u32[]{:S(2)}, u32[]{:S(2)}) collective-permute-start(bf16[2048,128]{1,0:T(8,128)(2,1)} %fusion.5), channel_id=1, source_target_pairs={{0,16},{16,0},{1,17},{17,1},{2,18},{18,2},{3,19},{19,3},{4,20},{20... | collective-permute-start | bytes 1572872 | tf_op jit(solution)/shard_map/ppermute | solution.py:515
  130.4 26.2 %collective-permute-start.4 = (bf16[512,512]{1,0:T(8,128)(2,1)S(1)}, bf16[512,512]{1,0:T(8,128)(2,1)S(1)}, u32[]{:S(2)}, u32[]{:S(2)}) collective-permute-start(bf16[512,512]{1,0:T(8,128)(2,1)S(1)} %get-tuple-element.190), channel_id=1, source_target_pairs={{0,2},{2,0},{1,3},{3,1},{4,6},{6,4},{5,7},{7,5},{8,10},{10,8},{9,1... | collective-permute-start | bytes 1572872 | tf_op jit(solution)/shard_map/ppermute | solution.py:513
  155.9 38.1 %collective-permute-start.23 = (bf16[512,1024]{1,0:T(8,128)(2,1)}, bf16[512,1024]{1,0:T(8,128)(2,1)S(1)}, u32[]{:S(2)}, u32[]{:S(2)}) collective-permute-start(bf16[512,1024]{1,0:T(8,128)(2,1)} %get-tuple-element.102), channel_id=1, source_target_pairs={{0,2},{2,0},{1,3},{3,1},{4,6},{6,4},{5,7},{7,5},{8,10},{10,8},{9,1... | collective-permute-start | bytes 3145736 | tf_op jit(solution)/shard_map/ppermute | solution.py:513
  186.8 14.9 %collective-permute-start.18 = (bf16[4,512,128]{2,1,0:T(8,128)(2,1)S(1)}, bf16[4,512,128]{2,1,0:T(8,128)(2,1)S(1)}, u32[]{:S(2)}, u32[]{:S(2)}) collective-permute-start(bf16[4,512,128]{2,1,0:T(8,128)(2,1)S(1)} %copy-done.82), channel_id=1, source_target_pairs={{0,2},{2,0},{1,3},{3,1},{4,6},{6,4},{5,7},{7,5},{8,10},{10,8},{9,1... | collective-permute-start | bytes 1572872 | tf_op jit(solution)/shard_map/ppermute | solution.py:513
  188.1 24.8 %collective-permute-start.17 = (bf16[4,512,128]{2,1,0:T(8,128)(2,1)S(1)}, bf16[4,512,128]{2,1,0:T(8,128)(2,1)S(1)}, u32[]{:S(2)}, u32[]{:S(2)}) collective-permute-start(bf16[4,512,128]{2,1,0:T(8,128)(2,1)S(1)} %copy-done.79), channel_id=1, source_target_pairs={{0,2},{2,0},{1,3},{3,1},{4,6},{6,4},{5,7},{7,5},{8,10},{10,8},{9,1... | collective-permute-start | bytes 1572872 | tf_op jit(solution)/shard_map/ppermute | solution.py:513
  194.0 70.0 %collective-permute-start.33 = (bf16[1024,1024]{1,0:T(8,128)(2,1)}, bf16[1024,1024]{1,0:T(8,128)(2,1)}, u32[]{:S(2)}, u32[]{:S(2)}) collective-permute-start(bf16[1024,1024]{1,0:T(8,128)(2,1)} %convolution_convert_fusion.1), channel_id=1, source_target_pairs={{0,1},{1,0},{2,3},{3,2},{4,5},{5,4},{6,7},{7,6},{8,9},{9,8},{10,11... | collective-permute-start | bytes 6291464 | tf_op jit(solution)/shard_map/ppermute | solution.py:514
  198.1 14.9 %copy-start = (f32[512,1024]{1,0:T(8,128)}, f32[512,1024]{1,0:T(8,128)S(1)}, u32[]{:S(2)}) copy-start(f32[512,1024]{1,0:T(8,128)S(1)} %get-tuple-element.111.dx_ref) | copy-start | bytes 6291460
  198.1 14.9 %copy-start.36 = (f32[8,1024]{1,0:T(8,128)}, f32[8,1024]{1,0:T(8,128)S(1)}, u32[]{:S(2)}) copy-start(f32[8,1024]{1,0:T(8,128)S(1)} %get-tuple-element.117) | copy-start | bytes 98308
  198.2 14.7 %copy-start.57 = (f32[4,512,128]{2,1,0:T(8,128)S(1)}, f32[4,512,128]{2,1,0:T(8,128)}, u32[]{:S(2)}) copy-start(f32[4,512,128]{2,1,0:T(8,128)} %get-tuple-element.92) | copy-start | bytes 3145732
  198.2 14.7 %copy-start.70 = (f32[1,512,1]{1,2,0:T(1,128)S(1)}, f32[1,512,1]{1,2,0:T(1,128)}, u32[]{:S(2)}) copy-start(f32[1,512,1]{1,2,0:T(1,128)} %get-tuple-element.228) | copy-start | bytes 6148
  201.6 18.2 %collective-permute-start.24 = (bf16[512,512]{1,0:T(8,128)(2,1)S(1)}, bf16[512,512]{1,0:T(8,128)(2,1)S(1)}, u32[]{:S(2)}, u32[]{:S(2)}) collective-permute-start(bf16[512,512]{1,0:T(8,128)(2,1)S(1)} %get-tuple-element.106), channel_id=1, source_target_pairs={{0,2},{2,0},{1,3},{3,1},{4,6},{6,4},{5,7},{7,5},{8,10},{10,8},{9,1... | collective-permute-start | bytes 1572872 | tf_op jit(solution)/shard_map/ppermute | solution.py:513
  212.9 56.9 %collective-permute-start.34 = (bf16[1024,1024]{1,0:T(8,128)(2,1)S(1)}, bf16[1024,1024]{1,0:T(8,128)(2,1)S(1)}, u32[]{:S(2)}, u32[]{:S(2)}) collective-permute-start(bf16[1024,1024]{1,0:T(8,128)(2,1)S(1)} %convolution_convert_fusion), channel_id=1, source_target_pairs={{0,1},{1,0},{2,3},{3,2},{4,5},{5,4},{6,7},{7,6},{8,9},{9,8},{10,11... | collective-permute-start | bytes 6291464 | tf_op jit(solution)/shard_map/ppermute | solution.py:514
  219.9 2.9 collective-permute-start.25
  222.8 38.9 %collective-permute-start.31 = (bf16[512,1024]{1,0:T(8,128)(2,1)}, bf16[512,1024]{1,0:T(8,128)(2,1)S(1)}, u32[]{:S(2)}, u32[]{:S(2)}) collective-permute-start(bf16[512,1024]{1,0:T(8,128)(2,1)} %convolution_convert_fusion.2), channel_id=1, source_target_pairs={{0,1},{1,0},{2,3},{3,2},{4,5},{5,4},{6,7},{7,6},{8,9},{9,8},{10,11... | collective-permute-start | bytes 3145736 | tf_op jit(solution)/shard_map/ppermute | solution.py:514
  223.6 32.7 %copy-start.64 = (bf16[2048,1024]{1,0:T(8,128)(2,1)S(1)}, bf16[2048,1024]{1,0:T(8,128)(2,1)}, u32[]{:S(2)}) copy-start(bf16[2048,1024]{1,0:T(8,128)(2,1)} %copy-done.63) | copy-start | bytes 12582916
  261.7 105.6 %collective-permute-start.29 = (bf16[4,512,128]{2,1,0:T(8,128)(2,1)}, bf16[4,512,128]{2,1,0:T(8,128)(2,1)}, u32[]{:S(2)}, u32[]{:S(2)}) collective-permute-start(bf16[4,512,128]{2,1,0:T(8,128)(2,1)} %get-tuple-element.178), channel_id=1, source_target_pairs={{0,2},{2,0},{1,3},{3,1},{4,6},{6,4},{5,7},{7,5},{8,10},{10,8},{9,1... | collective-permute-start | bytes 1572872 | tf_op jit(solution)/shard_map/ppermute | solution.py:513
  264.0 25.2 %collective-permute-start.19 = (bf16[2,1024,128]{2,1,0:T(8,128)(2,1)}, bf16[2,1024,128]{2,1,0:T(8,128)(2,1)}, u32[]{:S(2)}, u32[]{:S(2)}) collective-permute-start(bf16[2,1024,128]{2,1,0:T(8,128)(2,1)} %get-tuple-element.186), channel_id=1, source_target_pairs={{0,1},{1,0},{2,3},{3,2},{4,5},{5,4},{6,7},{7,6},{8,9},{9,8},{10,11... | collective-permute-start | bytes 1572872 | tf_op jit(solution)/shard_map/ppermute | solution.py:514
  269.8 17.7 %collective-permute-start.32 = (bf16[256,1024]{1,0:T(8,128)(2,1)S(1)}, bf16[256,1024]{1,0:T(8,128)(2,1)S(1)}, u32[]{:S(2)}, u32[]{:S(2)}) collective-permute-start(bf16[256,1024]{1,0:T(8,128)(2,1)S(1)} %slice.598), channel_id=1, source_target_pairs={{0,2},{2,0},{1,3},{3,1},{4,6},{6,4},{5,7},{7,5},{8,10},{10,8},{9,1... | collective-permute-start | bytes 1572872 | tf_op jit(solution)/shard_map/ppermute | solution.py:513
  289.1 3.4 collective-permute-start.30
  289.2 22.6 %copy-start.13 = (bf16[512,128]{1,0:T(8,128)(2,1)S(1)}, bf16[512,128]{1,0:T(8,128)(2,1)}, u32[]{:S(2)}) copy-start(bf16[512,128]{1,0:T(8,128)(2,1)} %get-tuple-element.209.refs_6_) | copy-start | bytes 393220
  289.2 22.6 %copy-start.38 = (s32[2,7]{1,0:T(2,128)S(1)}, s32[2,7]{1,0:T(2,128)}, u32[]{:S(2)}) copy-start(s32[2,7]{1,0:T(2,128)} %concatenate.70.shifts_ref) | copy-start | bytes 172
  289.2 22.6 %copy-start.39 = (s32[2,8]{1,0:T(2,128)S(1)}, s32[2,8]{1,0:T(2,128)}, u32[]{:S(2)}) copy-start(s32[2,8]{1,0:T(2,128)} %get-tuple-element.231.starts_ref) | copy-start | bytes 196
  289.2 22.6 %copy-start.40 = (s32[16]{0:T(128)S(1)}, s32[16]{0:T(128)}, u32[]{:S(2)}) copy-start(s32[16]{0:T(128)} %iota_multiply_fusion.2.out_pos_ref) | copy-start | bytes 196
  290.4 21.4 %collective-permute-start.21 = (bf16[2048,128]{1,0:T(8,128)(2,1)S(1)}, bf16[2048,128]{1,0:T(8,128)(2,1)S(1)}, u32[]{:S(2)}, u32[]{:S(2)}) collective-permute-start(bf16[2048,128]{1,0:T(8,128)(2,1)S(1)} %fusion.6), channel_id=1, source_target_pairs={{0,16},{16,0},{1,17},{17,1},{2,18},{18,2},{3,19},{19,3},{4,20},{20... | collective-permute-start | bytes 1572872 | tf_op jit(solution)/shard_map/ppermute | solution.py:515
  318.4 36.4 %collective-permute-start.26 = (bf16[3,1024,256]{2,1,0:T(8,128)(2,1)}, bf16[3,1024,256]{2,1,0:T(8,128)(2,1)}, u32[]{:S(2)}, u32[]{:S(2)}) collective-permute-start(bf16[3,1024,256]{2,1,0:T(8,128)(2,1)} %pad_maximum_fusion), channel_id=1, source_target_pairs={{0,1},{1,0},{2,3},{3,2},{4,5},{5,4},{6,7},{7,6},{8,9},{9,8},{10,11... | collective-permute-start | bytes 4718600 | tf_op jit(solution)/shard_map/ppermute | solution.py:514
  360.0 23.0 %collective-permute-start.28 = (bf16[512,1024]{1,0:T(8,128)(2,1)S(1)}, bf16[512,1024]{1,0:T(8,128)(2,1)S(1)}, u32[]{:S(2)}, u32[]{:S(2)}) collective-permute-start(bf16[512,1024]{1,0:T(8,128)(2,1)S(1)} %add_convert_fusion.2), channel_id=1, source_target_pairs={{0,2},{2,0},{1,3},{3,1},{4,6},{6,4},{5,7},{7,5},{8,10},{10,8},{9,1... | collective-permute-start | bytes 3145736 | tf_op jit(solution)/shard_map/ppermute | solution.py:513
  365.1 17.8 %copy-start.1 = (f32[512,1024]{1,0:T(8,128)S(1)}, f32[512,1024]{1,0:T(8,128)}, u32[]{:S(2)}) copy-start(f32[512,1024]{1,0:T(8,128)} %copy-done) | copy-start | bytes 6291460
  365.1 17.8 %copy-start.2 = (bf16[4,512,128]{2,1,0:T(8,128)(2,1)S(1)}, bf16[4,512,128]{2,1,0:T(8,128)(2,1)}, u32[]{:S(2)}) copy-start(bf16[4,512,128]{2,1,0:T(8,128)(2,1)} %get-tuple-element.179.gl_ref) | copy-start | bytes 1572868
  365.1 17.8 %copy-start.8 = (bf16[1,512,1,1024]{3,1,2,0:T(8,128)(2,1)S(1)}, bf16[1,512,1,1024]{3,1,2,0:T(8,128)(2,1)}, u32[]{:S(2)}) copy-start(bf16[1,512,1,1024]{3,1,2,0:T(8,128)(2,1)} %param.18) | copy-start | bytes 3145732
  (62 other events, 259.7 us)
Sparse Core Ops, SparseCore 0:
  288.6 218.9 all-reduce.4
